TPU v7x, 32 devices: a whole 2x2x4 slice. The times are simulated.
32 devices in a mesh: row: 4 (over x, core), col: 8 (over z, y).
Axes of the slice: x: 2, y: 2, z: 4, core: 2. Of those that a mesh axis runs over, the one named last changes fastest.
Arguments:
- p_valence: bfloat16 [4096, 4096], P('row', 'col'), as said below
- p_conduction: bfloat16 [4096, 4096], P('row', 'col'), as said below
- trial_vectors: bfloat16 [2, 4096, 4096], P(None, 'row', 'col'), may hold values from -6 to 6
- mask_valence: int32 [32, 32], replicated, may hold values from 0 to 1, as said below
- mask_conduction: int32 [32, 32], replicated, may hold values from 0 to 1, as said below
- mask_trial: int32 [32, 32], replicated, may hold values 0 or 1
- orbitals: bfloat16 [32, 128, 8192], P('row'), may hold values from -0.29882812 to 0.29882812
- sphere_starts: int32 [32], replicated, may hold values from 0 to 16, as said below
Outputs:
- kernel: bfloat16 [2, 4096, 4096], P(None, 'row', 'col')
- density: float32 [2, 16384], P(None, ('row', 'col'))
Inputs may be any that keep to these rules, and one draw needn't show every extreme that they name: `mask_valence`: symmetric, ones on the block diagonal and next to it. `mask_conduction`: symmetric, ones on the block diagonal and next to it. `p_valence`: symmetric. `p_conduction`: symmetric. `sphere_starts`: the first block's start is 0 and the last block's 32 - 16.
All inputs are finite; a program needn't handle non-finite values.
Results may differ from a plain program's by a relative error of at most 0.0049.
Values may be sent and summed in bfloat16 or wider, within the bound.
A program may use at most 320 MiB of HBM per device.

v0:
```python
import jax
import jax.numpy as jnp
from jax import lax
from jax.sharding import PartitionSpec as P

BS = 128
SPAN = 16
SP = 512


def broadcast(x, axis, root):
    mine = lax.axis_index(axis) == root
    return lax.psum(jnp.where(mine, x, jnp.zeros_like(x)), axis)


def masked(values, block_mask, row_index, col_index):
    leading_dims = values.shape[:-2]
    row_blocks = values.shape[-2] // BS
    col_blocks = values.shape[-1] // BS
    tile_mask = lax.dynamic_slice(
        block_mask, (row_index * row_blocks, col_index * col_blocks), (row_blocks, col_blocks)
    ).astype(values.dtype)
    shaped = values.reshape(leading_dims + (row_blocks, BS, col_blocks, BS))
    return (shaped * tile_mask[:, None, :, None]).reshape(values.shape)


def local(
    p_valence,
    p_conduction,
    trial_vectors,
    mask_valence,
    mask_conduction,
    mask_trial,
    orbitals,
    sphere_starts,
):
    row_index = lax.axis_index("row")
    col_index = lax.axis_index("col")
    valence = masked(p_valence, mask_valence, row_index, col_index)
    conduction = masked(p_conduction, mask_conduction, row_index, col_index)
    trials = masked(trial_vectors, mask_trial, row_index, col_index)
    vector_count = trials.shape[0]
    local_rows = trials.shape[1]
    local_cols = trials.shape[2]
    panels = lax.all_gather(trials, "col", axis=2, tiled=True)
    response = jnp.einsum(
        "vik,kj->vij",
        panels,
        lax.all_gather(conduction, "row", axis=0, tiled=True),
        preferred_element_type=jnp.float32,
    )
    response_half = response.astype(jnp.bfloat16)
    gathered = lax.all_gather(response_half, "row", axis=1, tiled=True)
    kernel_sum = jnp.einsum(
        "ik,vkj->vij",
        lax.all_gather(valence, "col", axis=1, tiled=True),
        gathered,
        preferred_element_type=jnp.float32,
    )
    kernel = masked(kernel_sum, mask_trial, row_index, col_index).astype(jnp.bfloat16)
    row_blocks = local_rows // BS
    col_blocks = local_cols // BS
    ratio = lax.axis_size("col") // lax.axis_size("row")
    own_part = lax.dynamic_slice_in_dim(orbitals, col_index % ratio * col_blocks, col_blocks, 0)
    partner = broadcast(own_part, "row", col_index // ratio)
    partner_padded = jnp.pad(
        partner.reshape(col_blocks, BS, SPAN, SP), ((0, 0), (0, 0), (SPAN, SPAN), (0, 0))
    )
    starts_rows = lax.dynamic_slice_in_dim(sphere_starts, row_index * row_blocks, row_blocks, 0)
    starts_cols = lax.dynamic_slice_in_dim(sphere_starts, col_index * col_blocks, col_blocks, 0)
    offsets = jnp.clip(starts_rows[:, None] - starts_cols[None, :] + SPAN, 0, 2 * SPAN)

    def take_frame(orbital_block, offset):
        return lax.dynamic_slice_in_dim(orbital_block, offset, SPAN, 1)

    def frames_for_row(offset_row):
        return jax.vmap(take_frame)(partner_padded, offset_row)

    frames = jax.vmap(frames_for_row)(offsets).reshape(row_blocks, col_blocks, BS, SPAN * SP)
    kernel_blocks = kernel.reshape(vector_count, row_blocks, BS, col_blocks, BS).transpose(
        0, 1, 3, 2, 4
    )
    applied = jnp.einsum(
        "vabmn,abnp->vamp", kernel_blocks, frames, preferred_element_type=jnp.float32
    )
    contrib = jnp.sum(orbitals[None] * applied, axis=2)
    slab_count = lax.axis_size("row") * lax.axis_size("col")
    density_grid = jnp.zeros((vector_count, slab_count, SP), jnp.float32)
    zero_index = jnp.zeros((), jnp.int32)
    for local_block in range(row_blocks):
        begin_slab = starts_rows[local_block]
        current = lax.dynamic_slice(
            density_grid, (zero_index, begin_slab, zero_index), (vector_count, SPAN, SP)
        )
        update = current + contrib[:, local_block].reshape(vector_count, SPAN, SP)
        density_grid = lax.dynamic_update_slice(
            density_grid, update, (zero_index, begin_slab, zero_index)
        )
    own_slab = lax.psum_scatter(density_grid, ("row", "col"), scatter_dimension=1, tiled=True)
    density = own_slab.reshape(vector_count, SP)
    return (kernel, density)


def solution(mesh):
    placed = (
        P("row", "col"),
        P("row", "col"),
        P(None, "row", "col"),
        P(),
        P(),
        P(),
        P("row", None, None),
        P(),
    )
    return jax.shard_map(
        local,
        mesh=mesh,
        in_specs=placed,
        out_specs=(P(None, "row", "col"), P(None, ("row", "col"))),
        check_vma=False,
    )
```

profile of v0, /device:TPU:0, one launch (start us, length us, event | category | flops | bytes accessed | tf_op | source)
XLA Modules:
  0.0 935.7 jit_solution(7683359424325019603)
XLA Ops:
  7.2 0.9 dynamic-slice_convert_fusion
  8.5 2.3 bitcast_multiply_fusion.3
  10.9 0.8 dynamic-slice_convert_fusion.2
  12.2 1.5 broadcast_multiply_fusion
  13.9 7.4 dynamic-slice_select_fusion
  21.2 11.8 %copy.28 = bf16[64,8,16,512]{3,2,1,0:T(8,128)(2,1)} copy(bf16[64,8,16,512]{3,1,2,0:T(8,128)(2,1)} %bitcast.123) | data formatting | bytes 16777216
  33.4 0.8 copy-done.2
  34.2 1.2 bitcast_multiply_fusion.2
  35.6 18.6 %convert_element_type.30 = f32[8,128,8192]{2,1,0:T(8,128)} convert(bf16[8,128,8192]{2,1,0:T(8,128)(2,1)} %param.14) | non-fusion elementwise | flops 8388608 | bytes 50331648 | tf_op jit(solution)/shard_map/convert_element_type | solution.py:86
  54.2 0.7 fusion.18
  65.0 213.2 %all-gather.5.cloned.1.call-done = bf16[2,1024,4096]{2,1,0:T(8,128)(2,1)} async-done(((bf16[2,1024,512]{2,1,0:T(8,128)(2,1)}), bf16[2,1024,4096]{2,1,0:T(8,128)(2,1)}) %all-gather.5.cloned.1.call-update) | async-done | bytes 16777232 | tf_op jit(solution)/shard_map/all_gather | solution.py:45
  278.2 14.5 %fusion.13 = bf16[2,1024,512]{2,1,0:T(8,128)(2,1)} fusion(bf16[2,1024,4096]{2,1,0:T(8,128)(2,1)} %all-gather.5.cloned.1.call-done, bf16[4096,512]{1,0:T(8,128)(2,1)} %all-gather.7.cloned.1.call-done), kind=kOutput, calls=%fused_computation.15 | convolution fusion | flops 8590983168 | bytes 23068672 | tf_op jit(solution)/shard_map/vik,kj->vij/dot_general | solution.py:46
  298.9 132.9 %all-reduce.5.cloned.1.call-done = bf16[4,128,16,512]{3,2,1,0:T(8,128)(2,1)} async-done(((bf16[4,128,16,512]{3,2,1,0:T(8,128)(2,1)}), bf16[4,128,16,512]{3,2,1,0:T(8,128)(2,1)}) %all-reduce.5.cloned.1.call-update) | async-done | bytes 8388624 | tf_op jit(solution)/shard_map/psum | solution.py:13
  431.8 12.1 %pad.4 = bf16[4,128,48,512]{3,2,1,0:T(8,128)(2,1)} pad(bf16[4,128,16,512]{3,2,1,0:T(8,128)(2,1)} %all-reduce.5.cloned.1.call-done, bf16[]{:T(256)} %constant.48.clone.1), padding=0_0x0_0x16_16x0_0 | pad | bytes 33554432 | tf_op jit(solution)/shard_map/jit(_pad)/pad | solution.py:66
  443.9 204.2 %while.1 = (s32[]{:T(128)}, bf16[4,128,48,512]{3,2,1,0:T(8,128)(2,1)}, s32[32,4]{0,1:T(4,128)S(1)}, bf16[32,128,16,512]{3,2,1,0:T(8,128)(2,1)}, s32[]{:T(128)}) while((s32[]{:T(128)}, bf16[4,128,48,512]{3,2,1,0:T(8,128)(2,1)}, s32[32,4]{0,1:T(4,128)S(1)}, bf16[32,128,16,512]{3,2,1,0:T(8,128)(2,1)}, s32[]{:T(128)}) %tuple.42), condition=%wide.while_cond, body=%wide.while_body.sunk | while | flops 2 | bytes 4195953 | solution.py:74
  444.0 0.6 fusion.22
  444.6 5.7 dynamic-slice_dynamic-update-slice_fusion.2
  450.4 0.6 fusion.22
  451.0 5.7 dynamic-slice_dynamic-update-slice_fusion.2
  457.3 5.8 dynamic-slice_dynamic-update-slice_fusion.2
  463.7 5.7 dynamic-slice_dynamic-update-slice_fusion.2
  469.5 0.6 fusion.22
  470.1 5.7 dynamic-slice_dynamic-update-slice_fusion.2
  476.5 5.7 dynamic-slice_dynamic-update-slice_fusion.2
  482.9 5.7 dynamic-slice_dynamic-update-slice_fusion.2
  488.7 0.6 fusion.22
  489.3 5.7 dynamic-slice_dynamic-update-slice_fusion.2
  495.1 0.6 fusion.22
  495.7 5.7 dynamic-slice_dynamic-update-slice_fusion.2
  501.5 0.6 fusion.22
  502.1 5.7 dynamic-slice_dynamic-update-slice_fusion.2
  508.4 5.7 dynamic-slice_dynamic-update-slice_fusion.2
  514.8 5.7 dynamic-slice_dynamic-update-slice_fusion.2
  521.2 5.7 dynamic-slice_dynamic-update-slice_fusion.2
  527.0 0.6 fusion.22
  527.6 5.7 dynamic-slice_dynamic-update-slice_fusion.2
  533.4 0.6 fusion.22
  534.0 5.8 dynamic-slice_dynamic-update-slice_fusion.2
  540.4 5.7 dynamic-slice_dynamic-update-slice_fusion.2
  546.7 5.7 dynamic-slice_dynamic-update-slice_fusion.2
  553.1 5.7 dynamic-slice_dynamic-update-slice_fusion.2
  559.5 5.7 dynamic-slice_dynamic-update-slice_fusion.2
  565.8 6.2 dynamic-slice_dynamic-update-slice_fusion.2
  572.7 5.7 dynamic-slice_dynamic-update-slice_fusion.2
  579.1 5.7 dynamic-slice_dynamic-update-slice_fusion.2
  585.4 5.7 dynamic-slice_dynamic-update-slice_fusion.2
  591.7 5.8 dynamic-slice_dynamic-update-slice_fusion.2
  598.2 5.7 dynamic-slice_dynamic-update-slice_fusion.2
  604.6 5.7 dynamic-slice_dynamic-update-slice_fusion.2
  611.0 5.7 dynamic-slice_dynamic-update-slice_fusion.2
  617.3 5.7 dynamic-slice_dynamic-update-slice_fusion.2
  623.7 5.4 dynamic-slice_dynamic-update-slice_fusion.2
  629.8 5.7 dynamic-slice_dynamic-update-slice_fusion.2
  636.1 5.7 dynamic-slice_dynamic-update-slice_fusion.2
  642.5 5.7 dynamic-slice_dynamic-update-slice_fusion.2
  648.1 98.3 %reshape.126 = bf16[8,4,128,8192,1]{3,2,1,0,4:T(8,128)(2,1)} reshape(bf16[32,128,16,512]{3,2,1,0:T(8,128)(2,1)} %get-tuple-element.9) | data formatting | bytes 134217728 | tf_op jit(solution)/shard_map/reshape | solution.py:79
  746.5 13.8 %fusion.7 = bf16[2,1024,512]{1,2,0:T(8,128)(2,1)S(1)} fusion(bf16[2,4096,512]{2,1,0:T(8,128)(2,1)} %all-gather.9.cloned.1.call-done, bf16[1024,4096]{1,0:T(8,128)(2,1)} %all-gather.11.cloned.1.call-done, f32[1024,512]{0,1:T(8,128)S(1)} %bitcast.131), kind=kOutput, calls=%fused_computation.10 | convolution fusion | flops 8592031744 | bytes 20971520 | tf_op jit(solution)/shard_map/ik,vkj->vij/dot_general | solution.py:54
  760.2 2.0 copy.29
  762.2 3.2 copy.18
  765.4 33.2 %fusion = f32[2,8,8192]{2,0,1:T(2,128)S(1)} fusion(f32[8,128,8192]{2,1,0:T(8,128)} %convert_element_type.30, bf16[8,4,128,8192,1]{3,2,1,0,4:T(8,128)(2,1)} %reshape.126, bf16[2,8,128,4,128]{4,2,3,0,1:T(8,128)(2,1)S(1)} %copy.18), kind=kOutput, calls=%fused_computation.3 | convolution fusion | flops 17213292544 | bytes 103284736 | tf_op jit(solution)/shard_map/vabmn,abnp->vamp/dot_general | solution.py:83
  801.5 0.7 copy.19
  802.3 3.9 copy.20
  806.3 121.3 %all-reduce.7.cloned.1.call-done = f32[2,32,512]{2,0,1:T(2,128)} async-done(((f32[2,32,512]{2,0,1:T(2,128)}), f32[2,32,512]{2,0,1:T(2,128)}) %all-reduce.7.cloned.1.call-update) | async-done | bytes 131088
  927.5 1.3 dynamic-slice_bitcast_fusion
  (111 shorter events, 22.2 us)
Async XLA Ops:
  7.2 5.1 copy-start.1
  7.2 57.8 %all-gather.7.cloned.1.call-start = ((), (), s32[]{:S(2)}) async-start(), calls=%async_computation.1 | async-start | bytes 5242880 | tf_op jit(solution)/shard_map/all_gather | solution.py:49
  10.9 267.3 %all-gather.5.cloned.1.call-start = ((), (), s32[]{:S(2)}) async-start(), calls=%async_computation | async-start | bytes 18874368 | tf_op jit(solution)/shard_map/all_gather | solution.py:45
  13.8 418.0 %all-reduce.5.cloned.1.call-start = ((), (), s32[]{:S(2)}) async-start(), calls=%async_computation.4 | async-start | bytes 16777216 | tf_op jit(solution)/shard_map/psum | solution.py:13
  33.0 1.2 copy-start.2
  33.0 2.5 copy-start.3
  33.0 713.4 %all-gather.11.cloned.1.call-start = ((), (), s32[]{:S(2)}) async-start(), calls=%async_computation.3 | async-start | bytes 9437184 | tf_op jit(solution)/shard_map/all_gather | solution.py:56
  35.4 711.0 %all-gather.9.cloned.1.call-start = ((), (), s32[]{:S(2)}) async-start(), calls=%async_computation.2 | async-start | bytes 10485760 | tf_op jit(solution)/shard_map/all_gather | solution.py:53
  292.8 634.8 %all-reduce.7.cloned.1.call-start = ((), (), s32[]{:S(2)}) async-start(), calls=%async_computation.5 | async-start | bytes 262144
  760.2 2.0 copy-start
Sparse Core Ops, SparseCore 0:
  11.0 37.2 all-gather.6
  50.9 227.2 all-gather.4
  280.7 151.0 all-reduce.4
  433.7 125.0 all-gather.10
  560.8 56.4 all-gather.8
  802.4 125.0 all-reduce.6
where the time goes:
time: 941 us; the launch traced here: 936 us
  waiting for transfers between devices  467 us (50%)
  local copies, waits for them, and re-layouts  344 us (37%)
  matrix products  61.5 us (7%)
  other arithmetic  32.9 us (3%)
  between operations  29.5 us (3%)
    all_gather x1, waiting for transfers between devices, local(): panels = lax.all_gather(trials, 'col', axis=2, tiled=True)  213 us
    gather x96, local copies, waits for them, and re-layouts  204 us
    psum x1, waiting for transfers between devices, broadcast(): return lax.psum(jnp.where(mine, x, jnp.zeros_like(x)), axis)  133 us
    unnamed x7, waiting for transfers between devices  121 us
    reshape x1, local copies, waits for them, and re-layouts, local(): jax.vmap(frames_for_row)(offsets)  98.3 us
    dot_general x1, matrix products, local(): jnp.einsum('vabmn,abnp->vamp', kernel_blocks, frames, preferred_element_t...  33.2 us
    unnamed x15, local copies, waits for them, and re-layouts  19.2 us
  transfers between devices with their start and end apart: 6, of which 3 were waited for; matrix products, arithmetic and copies ran while one was open for 40% of the time, Pallas kernels for 0%

commit v1 on v0

--- a/solution.py
+++ b/solution.py
@@ -1,6 +1,10 @@
+import functools
+
 import jax
 import jax.numpy as jnp
 from jax import lax
+from jax.experimental import pallas as pl
+from jax.experimental.pallas import tpu as pltpu
 from jax.sharding import PartitionSpec as P
 
 BS = 128
@@ -22,6 +26,67 @@
     ).astype(values.dtype)
     shaped = values.reshape(leading_dims + (row_blocks, BS, col_blocks, BS))
     return (shaped * tile_mask[:, None, :, None]).reshape(values.shape)
+
+
+def collocate_kernel(row_blocks, col_blocks, starts_rows, starts_cols, kernel_ref, *refs):
+    row_refs = refs[:row_blocks]
+    col_refs = refs[row_blocks : row_blocks + col_blocks]
+    out_ref, frame_ref = refs[row_blocks + col_blocks :]
+    slab = pl.program_id(0)
+    for j in range(col_blocks):
+        shift = slab - starts_cols[j]
+        active = (shift >= 0) & (shift < SPAN)
+
+        @pl.when(active)
+        def _():
+            frame_ref[j * BS : (j + 1) * BS, :] = col_refs[j][0]
+
+        @pl.when(jnp.logical_not(active))
+        def _():
+            frame_ref[j * BS : (j + 1) * BS, :] = jnp.zeros((BS, SP), frame_ref.dtype)
+
+    out_ref[...] = jnp.zeros_like(out_ref)
+    for i in range(row_blocks):
+        shift = slab - starts_rows[i]
+
+        @pl.when((shift >= 0) & (shift < SPAN))
+        def _():
+            own = row_refs[i][0].astype(jnp.float32)
+            for v in range(kernel_ref.shape[0]):
+                applied = jnp.dot(
+                    kernel_ref[v, i * BS : (i + 1) * BS, :],
+                    frame_ref[...],
+                    preferred_element_type=jnp.float32,
+                )
+                out_ref[0, v : v + 1, :] += jnp.sum(own * applied, axis=0, keepdims=True)
+
+
+def orbital_spec(block, which):
+    def index_map(slab, starts_rows, starts_cols):
+        start = (starts_rows, starts_cols)[which][block]
+        return block, 0, jnp.clip(slab - start, 0, SPAN - 1)
+
+    return pl.BlockSpec((1, BS, SP), index_map)
+
+
+def collocate(kernel, orbitals, partner, starts_rows, starts_cols, slab_count):
+    vector_count = kernel.shape[0]
+    row_blocks = orbitals.shape[0]
+    col_blocks = partner.shape[0]
+    return pl.pallas_call(
+        functools.partial(collocate_kernel, row_blocks, col_blocks),
+        out_shape=jax.ShapeDtypeStruct((slab_count, vector_count, SP), jnp.float32),
+        grid_spec=pltpu.PrefetchScalarGridSpec(
+            num_scalar_prefetch=2,
+            grid=(slab_count,),
+            in_specs=[pl.BlockSpec(kernel.shape, lambda slab, a, b: (0, 0, 0))]
+            + [orbital_spec(i, 0) for i in range(row_blocks)]
+            + [orbital_spec(j, 1) for j in range(col_blocks)],
+            out_specs=pl.BlockSpec((1, vector_count, SP), lambda slab, a, b: (slab, 0, 0)),
+            scratch_shapes=[pltpu.VMEM((col_blocks * BS, SP), jnp.bfloat16)],
+        ),
+        compiler_params=pltpu.CompilerParams(dimension_semantics=("arbitrary",)),
+    )(starts_rows, starts_cols, kernel, *([orbitals] * row_blocks), *([partner] * col_blocks))
 
 
 def local(
@@ -63,40 +128,11 @@
     ratio = lax.axis_size("col") // lax.axis_size("row")
     own_part = lax.dynamic_slice_in_dim(orbitals, col_index % ratio * col_blocks, col_blocks, 0)
     partner = broadcast(own_part, "row", col_index // ratio)
-    partner_padded = jnp.pad(
-        partner.reshape(col_blocks, BS, SPAN, SP), ((0, 0), (0, 0), (SPAN, SPAN), (0, 0))
-    )
     starts_rows = lax.dynamic_slice_in_dim(sphere_starts, row_index * row_blocks, row_blocks, 0)
     starts_cols = lax.dynamic_slice_in_dim(sphere_starts, col_index * col_blocks, col_blocks, 0)
-    offsets = jnp.clip(starts_rows[:, None] - starts_cols[None, :] + SPAN, 0, 2 * SPAN)
-
-    def take_frame(orbital_block, offset):
-        return lax.dynamic_slice_in_dim(orbital_block, offset, SPAN, 1)
-
-    def frames_for_row(offset_row):
-        return jax.vmap(take_frame)(partner_padded, offset_row)
-
-    frames = jax.vmap(frames_for_row)(offsets).reshape(row_blocks, col_blocks, BS, SPAN * SP)
-    kernel_blocks = kernel.reshape(vector_count, row_blocks, BS, col_blocks, BS).transpose(
-        0, 1, 3, 2, 4
-    )
-    applied = jnp.einsum(
-        "vabmn,abnp->vamp", kernel_blocks, frames, preferred_element_type=jnp.float32
-    )
-    contrib = jnp.sum(orbitals[None] * applied, axis=2)
     slab_count = lax.axis_size("row") * lax.axis_size("col")
-    density_grid = jnp.zeros((vector_count, slab_count, SP), jnp.float32)
-    zero_index = jnp.zeros((), jnp.int32)
-    for local_block in range(row_blocks):
-        begin_slab = starts_rows[local_block]
-        current = lax.dynamic_slice(
-            density_grid, (zero_index, begin_slab, zero_index), (vector_count, SPAN, SP)
-        )
-        update = current + contrib[:, local_block].reshape(vector_count, SPAN, SP)
-        density_grid = lax.dynamic_update_slice(
-            density_grid, update, (zero_index, begin_slab, zero_index)
-        )
-    own_slab = lax.psum_scatter(density_grid, ("row", "col"), scatter_dimension=1, tiled=True)
+    density_grid = collocate(kernel, orbitals, partner, starts_rows, starts_cols, slab_count)
+    own_slab = lax.psum_scatter(density_grid, ("row", "col"), scatter_dimension=0, tiled=True)
     density = own_slab.reshape(vector_count, SP)
     return (kernel, density)
 

time: 941 us -> 808 us (0.86)
  local copies, waits for them, and re-layouts: 344 us -> 4.63 us
  waiting for transfers between devices: 467 us -> 688 us
  Pallas kernels: 0 us -> 56.6 us
  matrix products: 61.5 us -> 29.3 us
  other arithmetic: 32.9 us -> 14 us
  between operations: 29.5 us -> 14.2 us
    gather x97 -> x0, local copies, waits for them, and re-layouts: 204 us -> none
    reshape x2 -> x0, local copies, waits for them, and re-layouts: 102 us -> none  [the longest x1 98.3 us: local(): jax.vmap(frames_for_row)(offsets)]
    all_gather x1, waiting for transfers between devices: 0.01 us -> 101 us  [local(): lax.all_gather(valence, 'col', axis=1, tiled=True)]
    all_gather x1, waiting for transfers between devices: 0.01 us -> 58.5 us  [local(): gathered = lax.all_gather(response_half, 'row', axis=1, tiled=True)]
    pallas_call x0 -> x1, Pallas kernels: none -> 56.6 us  [collocate(): pl.pallas_call(functools.partial(collocate_kernel, row_blocks, col_blocks...]
    dot_general x1 -> x0, matrix products: 33.2 us -> none  [local(): jnp.einsum('vabmn,abnp->vamp', kernel_blocks, frames, preferred_element_t...]
    all_gather x1, waiting for transfers between devices: 0.01 us -> 32.8 us  [local(): lax.all_gather(conduction, 'row', axis=0, tiled=True)]
    convert_element_type x1 -> x0, other arithmetic: 18.6 us -> none  [local(): contrib = jnp.sum(orbitals[None] * applied, axis=2)]
  transfers between devices with their start and end apart: 6 -> 6, of which waited for: 3 -> 6; matrix products, arithmetic and copies ran while one was open for 40% -> 5% of each run, Pallas kernels for 0% -> 0%
where the time goes in v1:
time: 808 us; the launch traced here: 807 us
  waiting for transfers between devices  688 us (85%)
  Pallas kernels  56.6 us (7%)
  matrix products  29.3 us (4%)
  between operations  14.2 us (2%)
  other arithmetic  14 us (2%)
    all_gather x1, waiting for transfers between devices, local(): panels = lax.all_gather(trials, 'col', axis=2, tiled=True)  230 us
    psum x1, waiting for transfers between devices, broadcast(): return lax.psum(jnp.where(mine, x, jnp.zeros_like(x)), axis)  141 us
    unnamed x7, waiting for transfers between devices  125 us
    all_gather x1, waiting for transfers between devices, local(): lax.all_gather(valence, 'col', axis=1, tiled=True)  101 us
    all_gather x1, waiting for transfers between devices, local(): gathered = lax.all_gather(response_half, 'row', axis=1, tiled=True)  58.5 us
    pallas_call x1, Pallas kernels, collocate(): pl.pallas_call(functools.partial(collocate_kernel, row_blocks, col_blocks...  56.6 us
    all_gather x1, waiting for transfers between devices, local(): lax.all_gather(conduction, 'row', axis=0, tiled=True)  32.8 us
  transfers between devices with their start and end apart: 6, of which 6 were waited for; matrix products, arithmetic and copies ran while one was open for 5% of the time, Pallas kernels for 0%

profile of v1, /device:TPU:0, one launch (start us, length us, event | category | flops | bytes accessed | tf_op | source)
XLA Modules:
  0.0 807.2 jit_solution(6044522908088302372)
XLA Ops:
  7.2 0.0 all-gather.7.cloned.1.call-start
  7.2 0.8 dynamic-slice_convert_fusion
  8.0 0.0 copy-start
  8.0 0.3 mul.71
  8.4 2.6 bitcast_multiply_fusion.2
  10.9 0.0 all-gather.7.cloned.1.call-update
  11.0 0.0 all-gather.5.cloned.1.call-start
  11.0 0.8 dynamic-slice_convert_fusion.2
  11.8 0.3 mul.67
  12.1 0.2 copy.22
  12.3 0.0 copy-done
  12.3 0.0 copy-start.1
  12.3 1.6 broadcast_multiply_fusion
  13.9 0.0 all-gather.5.cloned.1.call-update
  13.9 0.0 all-gather.11.cloned.1.call-start
  14.0 0.3 mul.74
  14.3 0.0 copy-done.1
  14.3 1.1 bitcast_multiply_fusion.1
  15.5 0.0 all-gather.11.cloned.1.call-update
  15.5 0.0 all-gather.9.cloned.1.call-start
  15.5 32.8 %all-gather.7.cloned.1.call-done = bf16[4096,512]{1,0:T(8,128)(2,1)} async-done(((bf16[1024,512]{1,0:T(8,128)(2,1)}), bf16[4096,512]{1,0:T(8,128)(2,1)}) %all-gather.7.cloned.1.call-update) | async-done | bytes 4194320 | tf_op jit(solution)/shard_map/all_gather | solution.py:114
  48.3 230.0 %all-gather.5.cloned.1.call-done = bf16[2,1024,4096]{2,1,0:T(8,128)(2,1)} async-done(((bf16[2,1024,512]{2,1,0:T(8,128)(2,1)}), bf16[2,1024,4096]{2,1,0:T(8,128)(2,1)}) %all-gather.5.cloned.1.call-update) | async-done | bytes 16777232 | tf_op jit(solution)/shard_map/all_gather | solution.py:110
  278.3 14.6 %fusion.7 = bf16[2,1024,512]{1,2,0:T(8,128)(2,1)} fusion(bf16[2,1024,4096]{2,1,0:T(8,128)(2,1)} %all-gather.5.cloned.1.call-done, bf16[4096,512]{1,0:T(8,128)(2,1)} %all-gather.7.cloned.1.call-done), kind=kOutput, calls=%fused_computation.8 | convolution fusion | flops 8590983168 | bytes 23068672 | tf_op jit(solution)/shard_map/vik,kj->vij/dot_general | solution.py:111
  292.9 0.0 all-gather.9.cloned.1.call-update
  292.9 0.0 all-reduce.4.cloned.1.call-start
  293.0 7.2 dynamic-slice_select_fusion
  300.2 0.0 copy-start.2
  300.2 0.0 all-reduce.4.cloned.1.call-update
  300.2 0.2 all-reduce.6.cloned.1.call-start
  300.4 0.4 copy-done.2
  300.8 0.7 dynamic_slice.23.starts_cols
  301.5 0.6 dynamic_slice.22.starts_rows
  302.1 0.3 mul.77
  302.4 0.2 copy.21
  302.6 100.9 %all-gather.11.cloned.1.call-done = bf16[1024,4096]{1,0:T(8,128)(2,1)} async-done(((bf16[1024,512]{1,0:T(8,128)(2,1)}), bf16[1024,4096]{1,0:T(8,128)(2,1)}) %all-gather.11.cloned.1.call-update) | async-done | bytes 8388624 | tf_op jit(solution)/shard_map/all_gather | solution.py:121
  403.5 58.5 %all-gather.9.cloned.1.call-done = bf16[2,4096,512]{1,2,0:T(8,128)(2,1)} async-done(((bf16[2,1024,512]{1,2,0:T(8,128)(2,1)}), bf16[2,4096,512]{1,2,0:T(8,128)(2,1)}) %all-gather.9.cloned.1.call-update) | async-done | bytes 8388624 | tf_op jit(solution)/shard_map/all_gather | solution.py:118
  462.0 14.7 %fusion.2.kernel_ref = bf16[2,1024,512]{2,1,0:T(8,128)(2,1)} fusion(bf16[2,4096,512]{1,2,0:T(8,128)(2,1)} %all-gather.9.cloned.1.call-done, bf16[1024,4096]{1,0:T(8,128)(2,1)} %all-gather.11.cloned.1.call-done, f32[1024,512]{1,0:T(8,128)S(1)} %bitcast.41), kind=kOutput, calls=%fused_computation.4 | convolution fusion | flops 8592031744 | bytes 20971520 | tf_op jit(solution)/shard_map/ik,vkj->vij/dot_general | solution.py:119
  476.7 140.5 %all-reduce.4.cloned.1.call-done.refs_8_.refs_9_.refs_10_.refs_11_ = bf16[4,128,8192]{2,1,0:T(8,128)(2,1)} async-done(((bf16[4,128,8192]{2,1,0:T(8,128)(2,1)}), bf16[4,128,8192]{2,1,0:T(8,128)(2,1)}) %all-reduce.4.cloned.1.call-update) | async-done | bytes 8388624 | tf_op jit(solution)/shard_map/psum | solution.py:17
  617.2 56.6 %shard_map.95 = f32[32,2,512]{2,1,0:T(2,128)} custom-call(s32[8]{0:T(128)} %dynamic_slice.22.starts_rows, s32[4]{0:T(128)} %dynamic_slice.23.starts_cols, bf16[2,1024,512]{2,1,0:T(8,128)(2,1)} %fusion.2.kernel_ref, bf16[8,128,8192]{2,1,0:T(8,128)(2,1)} %refs_7_.1, bf16[8,128,8192]{2,1,0:T(8,128)(2,1)} %refs_7_.1, bf16[8,128,8192]{2,1,0:T(8,128)(2,1)} %refs_7_.1, ...), custom_call_target="tpu_custom_call" | custom-call | tf_op jit(solution)/shard_map/pallas_call | solution.py:76
  673.8 0.0 all-reduce.6.cloned.1.call-update
  673.8 125.3 %all-reduce.6.cloned.1.call-done = f32[32,2,512]{2,1,0:T(2,128)} async-done(((f32[32,2,512]{2,1,0:T(2,128)}), f32[32,2,512]{2,1,0:T(2,128)}) %all-reduce.6.cloned.1.call-update) | async-done | bytes 131088
  799.1 1.3 dynamic-slice_bitcast_fusion
Async XLA Ops:
  7.2 41.2 %all-gather.7.cloned.1.call-start = ((), (), s32[]{:S(2)}) async-start(), calls=%async_computation.1 | async-start | bytes 5242880 | tf_op jit(solution)/shard_map/all_gather | solution.py:114
  8.0 4.3 copy-start
  11.0 267.3 %all-gather.5.cloned.1.call-start = ((), (), s32[]{:S(2)}) async-start(), calls=%async_computation | async-start | bytes 18874368 | tf_op jit(solution)/shard_map/all_gather | solution.py:110
  12.3 2.0 copy-start.1
  13.9 389.6 %all-gather.11.cloned.1.call-start = ((), (), s32[]{:S(2)}) async-start(), calls=%async_computation.3 | async-start | bytes 9437184 | tf_op jit(solution)/shard_map/all_gather | solution.py:121
  15.5 446.5 %all-gather.9.cloned.1.call-start = ((), (), s32[]{:S(2)}) async-start(), calls=%async_computation.2 | async-start | bytes 10485760 | tf_op jit(solution)/shard_map/all_gather | solution.py:118
  292.9 324.2 %all-reduce.4.cloned.1.call-start = ((), (), s32[]{:S(2)}) async-start(), calls=%async_computation.4 | async-start | bytes 16777216 | tf_op jit(solution)/shard_map/psum | solution.py:17
  300.2 0.7 copy-start.2
  300.2 498.9 %all-reduce.6.cloned.1.call-start = ((), (), s32[]{:S(2)}) async-start(), calls=%async_computation.5 | async-start | bytes 262144
Sparse Core Ops, SparseCore 0:
  11.1 37.2 all-gather.6
  51.0 227.2 all-gather.4
  280.3 123.1 all-gather.10
  405.5 56.4 all-gather.8
  464.3 152.8 all-reduce.3
  673.9 125.1 all-reduce.5

commit v2 on v1

--- a/solution.py
+++ b/solution.py
@@ -10,11 +10,6 @@
 BS = 128
 SPAN = 16
 SP = 512
-
-
-def broadcast(x, axis, root):
-    mine = lax.axis_index(axis) == root
-    return lax.psum(jnp.where(mine, x, jnp.zeros_like(x)), axis)
 
 
 def masked(values, block_mask, row_index, col_index):
@@ -89,6 +84,276 @@
     )(starts_rows, starts_cols, kernel, *([orbitals] * row_blocks), *([partner] * col_blocks))
 
 
+def ring_place(col, size):
+    odd = col % 2
+    return (col // 2) * (1 - odd) + (size - 1 - col // 2) * odd
+
+
+def ring_col(place, size):
+    far = place // (size // 2)
+    return 2 * place * (1 - far) + (2 * (size - 1 - place) + 1) * far
+
+
+def remote(src, dst, send_sem, recv_sem, **where):
+    return pltpu.make_async_remote_copy(
+        src_ref=src,
+        dst_ref=dst,
+        send_sem=send_sem,
+        recv_sem=recv_sem,
+        device_id=where,
+        device_id_type=pl.DeviceIdType.MESH,
+    )
+
+
+def ring_copy(mine, panel, place, size, step, way, send, recv):
+    rows, width = mine.shape[1] // 2, mine.shape[2]
+    sign = 1 - 2 * way
+    owner = ring_col((place - sign * step + size) % size, size)
+    half = pl.ds(way * rows, rows)
+    held = panel.at[:, half, pl.ds(pl.multiple_of(owner * width, width), width)]
+    src = mine.at[:, half, :] if step == 0 else held
+    target = ring_col((place + sign + size) % size, size)
+    return remote(src, held, send.at[way, step], recv.at[way, step], col=target)
+
+
+def row_part(stack, row, rows):
+    return stack.at[:, pl.ds(pl.multiple_of(row * rows, rows), rows), :]
+
+
+def gather_kernel(n_row, n_col, with_orbitals, *refs):
+    refs = list(refs)
+    ring_in, row_in = refs[:2]
+    del refs[:2]
+    orbitals = refs.pop(0) if with_orbitals else None
+    panel, stack = refs[:2]
+    del refs[:2]
+    partner = refs.pop(0) if with_orbitals else None
+    ring_hold, row_hold = refs[:2]
+    del refs[:2]
+    orbital_hold = refs.pop(0) if with_orbitals else None
+    hold_in, hold_out, ring_send, ring_recv, row_send, row_recv = refs[:6]
+    orbital_send, orbital_recv = refs[6:] if with_orbitals else (None, None)
+
+    row, col = lax.axis_index("row"), lax.axis_index("col")
+    place = ring_place(col, n_col)
+    chips = n_row // 2
+    chip, core = row // 2, row % 2
+    pair = row + 1 - 2 * core
+    rows, width = row_in.shape[1], ring_in.shape[2]
+
+    barrier = pltpu.get_barrier_semaphore()
+    for sign in (1, -1):
+        pl.semaphore_signal(
+            barrier,
+            inc=1,
+            device_id={"col": ring_col((place + sign + n_col) % n_col, n_col)},
+            device_id_type=pl.DeviceIdType.MESH,
+        )
+    for d in range(1, n_row):
+        pl.semaphore_signal(
+            barrier,
+            inc=1,
+            device_id={"row": (row + d) % n_row},
+            device_id_type=pl.DeviceIdType.MESH,
+        )
+    pl.semaphore_wait(barrier, n_row + 1)
+
+    def ring(step, way):
+        return ring_copy(ring_in, panel, place, n_col, step, way, ring_send, ring_recv)
+
+    def across(d):
+        target = pair if d == 0 else (chip + d) % chips * 2 + core
+        return remote(
+            row_in, row_part(stack, row, rows), row_send.at[d], row_recv.at[d], row=target
+        )
+
+    def onward(d):
+        held = row_part(stack, (chip - d + chips) % chips * 2 + core, rows)
+        k = chips - 1 + d
+        return remote(held, held, row_send.at[k], row_recv.at[k], row=pair)
+
+    ring(0, 0).start()
+    ring(0, 1).start()
+    for d in range(1, chips):
+        across(d).start()
+    across(0).start()
+
+    if with_orbitals:
+        blocks = partner.shape[0]
+        part = blocks // 2
+        ratio = n_col // n_row
+        source = col // ratio
+        own = orbitals.at[pl.ds(col % ratio * blocks, blocks)]
+        here = chip == source // 2
+        is_source = row == source
+
+        def to_pair():
+            return remote(own, partner, orbital_send.at[0], orbital_recv.at[0], row=pair)
+
+        def to_chip(d, h):
+            k = 1 + 2 * (d - 1) + h
+            return remote(
+                orbitals.at[pl.ds(col % ratio * blocks + h * part, part)],
+                partner.at[pl.ds(h * part, part)],
+                orbital_send.at[k],
+                orbital_recv.at[1],
+                row=(chip + d) % chips * 2 + h,
+            )
+
+        def half_onward():
+            held = partner.at[pl.ds(core * part, part)]
+            return remote(
+                held, held, orbital_send.at[2 * chips - 1], orbital_recv.at[2], row=pair
+            )
+
+        @pl.when(is_source)
+        def _():
+            for d in range(1, chips):
+                for h in range(2):
+                    to_chip(d, h).start()
+            to_pair().start()
+
+    ins = [(ring_in, ring_hold), (row_in, row_hold)]
+    outs = [
+        (ring_hold, panel.at[:, :, pl.ds(pl.multiple_of(col * width, width), width)]),
+        (row_hold, row_part(stack, row, rows)),
+    ]
+    for k in range(2):
+        pltpu.make_async_copy(*ins[k], hold_in.at[k]).start()
+    for k in range(2):
+        pltpu.make_async_copy(*ins[k], hold_in.at[k]).wait()
+        pltpu.make_async_copy(*outs[k], hold_out.at[k]).start()
+    if with_orbitals:
+
+        @pl.when(is_source)
+        def _():
+            fetch = pltpu.make_async_copy(own, orbital_hold, hold_in.at[2])
+            fetch.start()
+            fetch.wait()
+            pltpu.make_async_copy(orbital_hold, partner, hold_out.at[2]).start()
+
+    for step in range(n_col - 1):
+        for way in range(2):
+            ring(step, way).wait_recv()
+            if step < n_col - 2:
+                ring(step + 1, way).start()
+        if step == min(2, n_col - 2):
+            for d in range(1, chips):
+                across(d).wait_recv()
+                onward(d).start()
+        if with_orbitals and step == n_col - 3:
+
+            @pl.when(jnp.logical_not(here))
+            def _():
+                to_chip(1, 0).wait_recv()
+                half_onward().start()
+
+    across(0).wait_recv()
+    for d in range(1, chips):
+        onward(d).wait_recv()
+        onward(d).wait_send()
+        across(d).wait_send()
+    across(0).wait_send()
+    if with_orbitals:
+
+        @pl.when(is_source)
+        def _():
+            for d in range(1, chips):
+                for h in range(2):
+                    to_chip(d, h).wait_send()
+            to_pair().wait_send()
+            pltpu.make_async_copy(orbital_hold, partner, hold_out.at[2]).wait()
+
+        @pl.when(here & jnp.logical_not(is_source))
+        def _():
+            to_pair().wait_recv()
+
+        @pl.when(jnp.logical_not(here))
+        def _():
+            half_onward().wait_recv()
+            half_onward().wait_send()
+
+    for step in range(n_col - 1):
+        for way in range(2):
+            ring(step, way).wait_send()
+    for k in range(2):
+        pltpu.make_async_copy(*outs[k], hold_out.at[k]).wait()
+
+
+def gather(ring_in, row_in, orbitals, collective_id):
+    n_row, n_col = lax.axis_size("row"), lax.axis_size("col")
+    lead, rows, width = ring_in.shape
+    panel = jax.ShapeDtypeStruct((lead, rows, n_col * width), ring_in.dtype)
+    stack = jax.ShapeDtypeStruct(
+        (row_in.shape[0], n_row * row_in.shape[1], row_in.shape[2]), row_in.dtype
+    )
+    operands, results = [ring_in, row_in], [panel, stack]
+    holds = [pltpu.VMEM(ring_in.shape, ring_in.dtype), pltpu.VMEM(row_in.shape, row_in.dtype)]
+    dma = pltpu.SemaphoreType.DMA
+    sems = [dma((3,)), dma((3,)), dma((2, n_col - 1)), dma((2, n_col - 1))]
+    sems += [dma((n_row - 1,)), dma((n_row - 1,))]
+    if orbitals is not None:
+        blocks = orbitals.shape[0] * n_row // n_col
+        partner = (blocks,) + orbitals.shape[1:]
+        operands.append(orbitals)
+        results.append(jax.ShapeDtypeStruct(partner, orbitals.dtype))
+        holds.append(pltpu.VMEM(partner, orbitals.dtype))
+        sems += [dma((n_row,)), dma((3,))]
+    return pl.pallas_call(
+        functools.partial(gather_kernel, n_row, n_col, orbitals is not None),
+        out_shape=results,
+        in_specs=[pl.BlockSpec(memory_space=pl.ANY)] * len(operands),
+        out_specs=[pl.BlockSpec(memory_space=pl.ANY)] * len(results),
+        scratch_shapes=holds + sems,
+        compiler_params=pltpu.CompilerParams(
+            collective_id=collective_id, has_side_effects=True
+        ),
+    )(*operands)
+
+
+def reduce_kernel(axis, size, in_ref, out_ref, landed, own_sem, send, recv):
+    me = lax.axis_index(axis)
+    barrier = pltpu.get_barrier_semaphore()
+    for d in range(1, size):
+        pl.semaphore_signal(
+            barrier,
+            inc=1,
+            device_id={axis: (me + d) % size},
+            device_id_type=pl.DeviceIdType.MESH,
+        )
+    own = pltpu.make_async_copy(in_ref.at[me], landed.at[0], own_sem)
+    own.start()
+    pl.semaphore_wait(barrier, size - 1)
+    copies = []
+    for d in range(1, size):
+        target = (me + d) % size
+        copies.append(
+            remote(in_ref.at[target], landed.at[d], send.at[d], recv.at[d], **{axis: target})
+        )
+        copies[-1].start()
+    own.wait()
+    for copy in copies:
+        copy.wait_recv()
+    out_ref[...] = jnp.sum(landed[...], axis=0)
+    for copy in copies:
+        copy.wait_send()
+
+
+def reduce_over(axis, terms, collective_id):
+    size = terms.shape[0]
+    dma = pltpu.SemaphoreType.DMA
+    return pl.pallas_call(
+        functools.partial(reduce_kernel, axis, size),
+        out_shape=jax.ShapeDtypeStruct(terms.shape[1:], terms.dtype),
+        in_specs=[pl.BlockSpec(memory_space=pl.ANY)],
+        out_specs=pl.BlockSpec(memory_space=pltpu.VMEM),
+        scratch_shapes=[pltpu.VMEM(terms.shape, terms.dtype), dma, dma((size,)), dma((size,))],
+        compiler_params=pltpu.CompilerParams(
+            collective_id=collective_id, has_side_effects=True
+        ),
+    )(terms)
+
+
 def local(
     p_valence,
     p_conduction,
@@ -107,33 +372,24 @@
     vector_count = trials.shape[0]
     local_rows = trials.shape[1]
     local_cols = trials.shape[2]
-    panels = lax.all_gather(trials, "col", axis=2, tiled=True)
+    panels, conduction_cols, partner = gather(trials, conduction[None], orbitals, 0)
     response = jnp.einsum(
-        "vik,kj->vij",
-        panels,
-        lax.all_gather(conduction, "row", axis=0, tiled=True),
-        preferred_element_type=jnp.float32,
-    )
-    response_half = response.astype(jnp.bfloat16)
-    gathered = lax.all_gather(response_half, "row", axis=1, tiled=True)
+        "vik,kj->vij", panels, conduction_cols[0], preferred_element_type=jnp.float32
+    ).astype(jnp.bfloat16)
+    valence_rows, gathered = gather(valence[None], response, None, 1)
     kernel_sum = jnp.einsum(
-        "ik,vkj->vij",
-        lax.all_gather(valence, "col", axis=1, tiled=True),
-        gathered,
-        preferred_element_type=jnp.float32,
+        "ik,vkj->vij", valence_rows[0], gathered, preferred_element_type=jnp.float32
     )
     kernel = masked(kernel_sum, mask_trial, row_index, col_index).astype(jnp.bfloat16)
     row_blocks = local_rows // BS
     col_blocks = local_cols // BS
-    ratio = lax.axis_size("col") // lax.axis_size("row")
-    own_part = lax.dynamic_slice_in_dim(orbitals, col_index % ratio * col_blocks, col_blocks, 0)
-    partner = broadcast(own_part, "row", col_index // ratio)
     starts_rows = lax.dynamic_slice_in_dim(sphere_starts, row_index * row_blocks, row_blocks, 0)
     starts_cols = lax.dynamic_slice_in_dim(sphere_starts, col_index * col_blocks, col_blocks, 0)
     slab_count = lax.axis_size("row") * lax.axis_size("col")
     density_grid = collocate(kernel, orbitals, partner, starts_rows, starts_cols, slab_count)
-    own_slab = lax.psum_scatter(density_grid, ("row", "col"), scatter_dimension=0, tiled=True)
-    density = own_slab.reshape(vector_count, SP)
+    n_row, n_col = lax.axis_size("row"), lax.axis_size("col")
+    terms = density_grid.reshape(n_row, n_col, vector_count, SP)
+    density = reduce_over("col", reduce_over("row", terms, 2), 3)
     return (kernel, density)
 
 

time: 808 us -> 363 us (0.45)
  waiting for transfers between devices: 688 us -> 0 us
  Pallas kernels: 56.6 us -> 323 us
  between operations: 14.2 us -> 0.77 us
  other arithmetic: 14 us -> 5.65 us
    all_gather x4 -> x0, waiting for transfers between devices: 422 us -> none  [the longest x1 230 us: local(): panels = lax.all_gather(trials, 'col', axis=2, tiled=True)]
    pallas_call x0 -> x4, Pallas kernels: none -> 266 us  [the longest x2 253 us: gather(): pl.pallas_call(functools.partial(gather_kernel, n_row, n_col, orbitals is...]
    psum x1 -> x0, waiting for transfers between devices: 141 us -> none  [broadcast(): return lax.psum(jnp.where(mine, x, jnp.zeros_like(x)), axis)]
    unnamed x7 -> x0, waiting for transfers between devices: 125 us -> none
  transfers between devices with their start and end apart: 6 -> 0, of which waited for: 6 -> 0; matrix products, arithmetic and copies ran while one was open for 5% -> 0% of each run, Pallas kernels for 0% -> 0%
where the time goes in v2:
time: 363 us
  Pallas kernels  323 us (89%)
  matrix products  29.3 us (8%)
  other arithmetic  5.65 us (2%)
  local copies, waits for them, and re-layouts  4.34 us (1%)
    pallas_call x2, Pallas kernels, gather(): pl.pallas_call(functools.partial(gather_kernel, n_row, n_col, orbitals is...  253 us
    pallas_call x1, Pallas kernels, collocate(): pl.pallas_call(functools.partial(collocate_kernel, row_blocks, col_blocks...  56.5 us
    dot_general x1, matrix products, local(): jnp.einsum('ik,vkj->vij', valence_rows[0], gathered, preferred_element_ty...  14.6 us
    dot_general x1, matrix products, local(): jnp.einsum('vik,kj->vij', panels, conduction_cols[0], preferred_element_t...  14.6 us
    pallas_call x2, Pallas kernels, reduce_over(): pl.pallas_call(functools.partial(reduce_kernel, axis, size), out_shape=ja...  13.6 us

profile of v2, /device:TPU:0, one launch (start us, length us, event | category | flops | bytes accessed | tf_op | source)
XLA Modules:
  0.0 362.8 jit_solution(3484431533350006442)
XLA Ops:
  0.6 0.0 copy-start
  0.6 0.9 dynamic-slice_convert_fusion.2
  1.6 0.3 mul.74
  1.9 0.0 copy-start.1
  1.9 0.2 copy.23
  2.1 0.1 copy-done
  2.2 1.5 broadcast_multiply_fusion.refs_0_
  3.8 0.8 dynamic-slice_convert_fusion
  4.5 0.3 mul.78
  4.9 0.0 copy-done.1
  4.9 1.2 fusion.10.refs_1_
  6.1 168.6 %shard_map.95 = (bf16[2,1024,4096]{2,1,0:T(8,128)(2,1)}, bf16[1,4096,512]{2,1,0:T(8,128)(2,1)}, bf16[4,128,8192]{2,1,0:T(8,128)(2,1)}) custom-call(bf16[2,1024,512]{2,1,0:T(8,128)(2,1)} %broadcast_multiply_fusion.refs_0_, bf16[1,1024,512]{2,1,0:T(8,128)(2,1)} %fusion.10.refs_1_, bf16[8,128,8192]{2,1,0:T(8,128)(2,1)} %refs_7_.1), custom_call_target="tpu_custom_call" | custom-call | tf_op jit(solution)/shard_map/pallas_call | solution.py:302
  174.7 0.0 copy-start.2
  174.7 14.6 %fusion.7.refs_1_ = bf16[2,1024,512]{2,1,0:T(8,128)(2,1)} fusion(bf16[2,1024,4096]{2,1,0:T(8,128)(2,1)} %get-tuple-element.7, bf16[1,4096,512]{2,1,0:T(8,128)(2,1)} %get-tuple-element.8), kind=kOutput, calls=%fused_computation.7 | convolution fusion | flops 8590983168 | bytes 23068672 | tf_op jit(solution)/shard_map/vik,kj->vij/dot_general | solution.py:376
  189.4 0.3 mul.70
  189.7 0.0 copy-done.2
  189.7 1.2 fusion.11.refs_0_
  191.0 84.0 %shard_map.96 = (bf16[1,1024,4096]{2,1,0:T(8,128)(2,1)}, bf16[2,4096,512]{2,1,0:T(8,128)(2,1)}) custom-call(bf16[1,1024,512]{2,1,0:T(8,128)(2,1)} %fusion.11.refs_0_, bf16[2,1024,512]{2,1,0:T(8,128)(2,1)} %fusion.7.refs_1_), custom_call_target="tpu_custom_call" | custom-call | tf_op jit(solution)/shard_map/pallas_call | solution.py:302
  275.0 0.3 mul.82
  275.4 0.2 copy.22
  275.5 0.0 copy-start.3
  275.6 14.6 %fusion.2.kernel_ref = bf16[2,1024,512]{2,1,0:T(8,128)(2,1)} fusion(bf16[2,4096,512]{2,1,0:T(8,128)(2,1)} %get-tuple-element.9, bf16[1,1024,4096]{2,1,0:T(8,128)(2,1)} %get-tuple-element.10, f32[1024,512]{1,0:T(8,128)S(1)} %bitcast.50), kind=kOutput, calls=%fused_computation.3 | convolution fusion | flops 8592031744 | bytes 20971520 | tf_op jit(solution)/shard_map/ik,vkj->vij/dot_general | solution.py:380
  290.2 0.0 copy-done.3
  290.2 0.6 dynamic_slice.20.starts_cols
  290.8 0.6 dynamic_slice.19.starts_rows
  291.4 56.5 %shard_map.97 = f32[32,2,512]{2,1,0:T(2,128)} custom-call(s32[8]{0:T(128)} %dynamic_slice.19.starts_rows, s32[4]{0:T(128)} %dynamic_slice.20.starts_cols, bf16[2,1024,512]{2,1,0:T(8,128)(2,1)} %fusion.2.kernel_ref, bf16[8,128,8192]{2,1,0:T(8,128)(2,1)} %refs_7_.1, bf16[8,128,8192]{2,1,0:T(8,128)(2,1)} %refs_7_.1, bf16[8,128,8192]{2,1,0:T(8,128)(2,1)} %refs_7_.1, ...), custom_call_target="tpu_custom_call" | custom-call | tf_op jit(solution)/shard_map/pallas_call | solution.py:71
  347.9 6.2 %shard_map.98.in_ref = f32[8,2,512]{2,1,0:T(2,128)} custom-call(f32[4,8,2,512]{3,2,1,0:T(2,128)} %bitcast.51), custom_call_target="tpu_custom_call" | custom-call | tf_op jit(solution)/shard_map/pallas_call | solution.py:345
  354.1 7.5 %shard_map.99 = f32[2,512]{1,0:T(2,128)} custom-call(f32[8,2,512]{2,1,0:T(2,128)} %shard_map.98.in_ref), custom_call_target="tpu_custom_call" | custom-call | tf_op jit(solution)/shard_map/pallas_call | solution.py:345
  361.6 1.3 copy.25
Async XLA Ops:
  0.6 1.6 copy-start
  1.9 3.0 copy-start.1
  174.7 15.0 %copy-start.2 = (bf16[1024,512]{1,0:T(8,128)(2,1)S(1)}, bf16[1024,512]{1,0:T(8,128)(2,1)}, u32[]{:S(2)}) copy-start(bf16[1024,512]{1,0:T(8,128)(2,1)} %param.8) | copy-start | bytes 3145732
  275.5 14.7 %copy-start.3 = (s32[32]{0:T(128)S(1)}, s32[32]{0:T(128)}, u32[]{:S(2)}) copy-start(s32[32]{0:T(128)} %param.15) | copy-start | bytes 388

commit v3 on v2

--- a/solution.py
+++ b/solution.py
@@ -47,13 +47,12 @@
         @pl.when((shift >= 0) & (shift < SPAN))
         def _():
             own = row_refs[i][0].astype(jnp.float32)
-            for v in range(kernel_ref.shape[0]):
-                applied = jnp.dot(
-                    kernel_ref[v, i * BS : (i + 1) * BS, :],
-                    frame_ref[...],
-                    preferred_element_type=jnp.float32,
-                )
-                out_ref[0, v : v + 1, :] += jnp.sum(own * applied, axis=0, keepdims=True)
+            vectors = kernel_ref.shape[0]
+            left = kernel_ref[:, i * BS : (i + 1) * BS, :].reshape(vectors * BS, col_blocks * BS)
+            applied = jnp.dot(left, frame_ref[...], preferred_element_type=jnp.float32)
+            for v in range(vectors):
+                term = own * applied[v * BS : (v + 1) * BS]
+                out_ref[0, v : v + 1, :] += jnp.sum(term, axis=0, keepdims=True)
 
 
 def orbital_spec(block, which):
@@ -105,12 +104,12 @@
     )
 
 
-def ring_copy(mine, panel, place, size, step, way, send, recv):
-    rows, width = mine.shape[1] // 2, mine.shape[2]
+def ring_copy(mine, panel, used, place, size, step, way, send, recv):
+    rows = used // 2
     sign = 1 - 2 * way
     owner = ring_col((place - sign * step + size) % size, size)
     half = pl.ds(way * rows, rows)
-    held = panel.at[:, half, pl.ds(pl.multiple_of(owner * width, width), width)]
+    held = panel.at[owner, :, half, :]
     src = mine.at[:, half, :] if step == 0 else held
     target = ring_col((place + sign + size) % size, size)
     return remote(src, held, send.at[way, step], recv.at[way, step], col=target)
@@ -120,7 +119,7 @@
     return stack.at[:, pl.ds(pl.multiple_of(row * rows, rows), rows), :]
 
 
-def gather_kernel(n_row, n_col, with_orbitals, *refs):
+def gather_kernel(n_row, n_col, used, with_orbitals, *refs):
     refs = list(refs)
     ring_in, row_in = refs[:2]
     del refs[:2]
@@ -139,7 +138,7 @@
     chips = n_row // 2
     chip, core = row // 2, row % 2
     pair = row + 1 - 2 * core
-    rows, width = row_in.shape[1], ring_in.shape[2]
+    rows = row_in.shape[1]
 
     barrier = pltpu.get_barrier_semaphore()
     for sign in (1, -1):
@@ -159,7 +158,7 @@
     pl.semaphore_wait(barrier, n_row + 1)
 
     def ring(step, way):
-        return ring_copy(ring_in, panel, place, n_col, step, way, ring_send, ring_recv)
+        return ring_copy(ring_in, panel, used, place, n_col, step, way, ring_send, ring_recv)
 
     def across(d):
         target = pair if d == 0 else (chip + d) % chips * 2 + core
@@ -213,9 +212,9 @@
                     to_chip(d, h).start()
             to_pair().start()
 
-    ins = [(ring_in, ring_hold), (row_in, row_hold)]
+    ins = [(ring_in.at[:, pl.ds(0, used), :], ring_hold), (row_in, row_hold)]
     outs = [
-        (ring_hold, panel.at[:, :, pl.ds(pl.multiple_of(col * width, width), width)]),
+        (ring_hold, panel.at[col, :, pl.ds(0, used), :]),
         (row_hold, row_part(stack, row, rows)),
     ]
     for k in range(2):
@@ -280,15 +279,25 @@
         pltpu.make_async_copy(*outs[k], hold_out.at[k]).wait()
 
 
-def gather(ring_in, row_in, orbitals, collective_id):
+def gather(fractions, largest, first_id, *arrays):
+    slots = arrays[0].shape[1] // BS
+    caps = sorted({-(-slots * part // 16) for part in fractions})
+    branches = [
+        functools.partial(gather_slots, cap * BS, first_id + k) for k, cap in enumerate(caps)
+    ]
+    index = sum((largest > cap).astype(jnp.int32) for cap in caps[:-1])
+    return lax.switch(index, branches, *arrays)
+
+
+def gather_slots(used, collective_id, ring_in, row_in, orbitals=None):
     n_row, n_col = lax.axis_size("row"), lax.axis_size("col")
-    lead, rows, width = ring_in.shape
-    panel = jax.ShapeDtypeStruct((lead, rows, n_col * width), ring_in.dtype)
+    panel = jax.ShapeDtypeStruct((n_col,) + ring_in.shape, ring_in.dtype)
     stack = jax.ShapeDtypeStruct(
         (row_in.shape[0], n_row * row_in.shape[1], row_in.shape[2]), row_in.dtype
     )
     operands, results = [ring_in, row_in], [panel, stack]
-    holds = [pltpu.VMEM(ring_in.shape, ring_in.dtype), pltpu.VMEM(row_in.shape, row_in.dtype)]
+    hold = (ring_in.shape[0], used, ring_in.shape[2])
+    holds = [pltpu.VMEM(hold, ring_in.dtype), pltpu.VMEM(row_in.shape, row_in.dtype)]
     dma = pltpu.SemaphoreType.DMA
     sems = [dma((3,)), dma((3,)), dma((2, n_col - 1)), dma((2, n_col - 1))]
     sems += [dma((n_row - 1,)), dma((n_row - 1,))]
@@ -300,7 +309,7 @@
         holds.append(pltpu.VMEM(partner, orbitals.dtype))
         sems += [dma((n_row,)), dma((3,))]
     return pl.pallas_call(
-        functools.partial(gather_kernel, n_row, n_col, orbitals is not None),
+        functools.partial(gather_kernel, n_row, n_col, used, orbitals is not None),
         out_shape=results,
         in_specs=[pl.BlockSpec(memory_space=pl.ANY)] * len(operands),
         out_specs=[pl.BlockSpec(memory_space=pl.ANY)] * len(results),
@@ -354,6 +363,120 @@
     )(terms)
 
 
+def block_slots(block_mask, row_index, row_blocks, col_blocks):
+    tiles = lax.dynamic_slice_in_dim(block_mask, row_index * row_blocks, row_blocks, 0)
+    tiles = tiles.reshape(row_blocks, -1, col_blocks).transpose(1, 0, 2)
+    tiles = tiles.reshape(tiles.shape[0], row_blocks * col_blocks)
+    return jnp.where(tiles > 0, jnp.cumsum(tiles, axis=1) - 1, -1).astype(jnp.int32)
+
+
+def largest_count(block_mask, row_blocks, col_blocks):
+    rows, cols = block_mask.shape
+    tiles = block_mask.reshape(rows // row_blocks, row_blocks, cols // col_blocks, col_blocks)
+    return jnp.max(jnp.sum(tiles, axis=(1, 3)))
+
+
+def pack_kernel(slots, values_ref, out_ref):
+    col_blocks = values_ref.shape[2] // BS
+    for k in range(out_ref.shape[1] // BS):
+        a, b = divmod(k, col_blocks)
+
+        @pl.when(slots[k] >= 0)
+        def _():
+            start = pl.multiple_of(slots[k] * BS, BS)
+            out_ref[:, pl.ds(start, BS), :] = values_ref[
+                :, a * BS : (a + 1) * BS, b * BS : (b + 1) * BS
+            ]
+
+
+def pack(values, slots):
+    lead, rows, cols = values.shape
+    return pl.pallas_call(
+        pack_kernel,
+        out_shape=jax.ShapeDtypeStruct((lead, rows * cols // BS, BS), values.dtype),
+        in_specs=[
+            pl.BlockSpec(memory_space=pltpu.SMEM),
+            pl.BlockSpec(memory_space=pltpu.VMEM),
+        ],
+        out_specs=pl.BlockSpec(memory_space=pltpu.VMEM),
+    )(slots, values)
+
+
+def product_kernel(slots, keep, left_ref, right_ref, out_ref, dense, total):
+    step = pl.program_id(0)
+    rows, depth = dense.shape[1:]
+    col_blocks = depth // BS
+    count = rows // BS * col_blocks
+    for k in range(count):
+        a, b = divmod(k, col_blocks)
+        slot = slots[step * count + k]
+
+        @pl.when(slot >= 0)
+        def _():
+            start = pl.multiple_of(slot * BS, BS)
+            dense[:, a * BS : (a + 1) * BS, b * BS : (b + 1) * BS] = left_ref[
+                0, :, pl.ds(start, BS), :
+            ]
+
+        @pl.when(slot < 0)
+        def _():
+            dense[:, a * BS : (a + 1) * BS, b * BS : (b + 1) * BS] = jnp.zeros(
+                (dense.shape[0], BS, BS), dense.dtype
+            )
+
+    for v in range(total.shape[0]):
+        term = jnp.dot(
+            dense[min(v, dense.shape[0] - 1)],
+            right_ref[min(v, right_ref.shape[0] - 1)],
+            preferred_element_type=jnp.float32,
+        )
+
+        @pl.when(step == 0)
+        def _():
+            total[v] = term
+
+        @pl.when(step > 0)
+        def _():
+            total[v] += term
+
+    @pl.when(step == pl.num_programs(0) - 1)
+    def _():
+        wide = out_ref.shape[2] // BS
+        for a in range(rows // BS):
+            for b in range(wide):
+                block = total[:, a * BS : (a + 1) * BS, b * BS : (b + 1) * BS]
+                block = block * keep[a * wide + b].astype(jnp.float32)
+                out_ref[:, a * BS : (a + 1) * BS, b * BS : (b + 1) * BS] = block.astype(
+                    out_ref.dtype
+                )
+
+
+def product(panel, slots, right, keep):
+    steps, lead, packed, _ = panel.shape
+    depth = right.shape[1] // steps
+    rows = packed * BS // depth
+    width = right.shape[2]
+    vectors = max(lead, right.shape[0])
+    return pl.pallas_call(
+        product_kernel,
+        out_shape=jax.ShapeDtypeStruct((vectors, rows, width), panel.dtype),
+        grid_spec=pltpu.PrefetchScalarGridSpec(
+            num_scalar_prefetch=2,
+            grid=(steps,),
+            in_specs=[
+                pl.BlockSpec((1, lead, packed, BS), lambda c, a, b: (c, 0, 0, 0)),
+                pl.BlockSpec((right.shape[0], depth, width), lambda c, a, b: (0, c, 0)),
+            ],
+            out_specs=pl.BlockSpec((vectors, rows, width), lambda c, a, b: (0, 0, 0)),
+            scratch_shapes=[
+                pltpu.VMEM((lead, rows, depth), panel.dtype),
+                pltpu.VMEM((vectors, rows, width), jnp.float32),
+            ],
+        ),
+        compiler_params=pltpu.CompilerParams(dimension_semantics=("arbitrary",)),
+    )(slots.reshape(-1), keep.reshape(-1), panel, right)
+
+
 def local(
     p_valence,
     p_conduction,
@@ -366,30 +489,32 @@
 ):
     row_index = lax.axis_index("row")
     col_index = lax.axis_index("col")
-    valence = masked(p_valence, mask_valence, row_index, col_index)
-    conduction = masked(p_conduction, mask_conduction, row_index, col_index)
-    trials = masked(trial_vectors, mask_trial, row_index, col_index)
-    vector_count = trials.shape[0]
-    local_rows = trials.shape[1]
-    local_cols = trials.shape[2]
-    panels, conduction_cols, partner = gather(trials, conduction[None], orbitals, 0)
-    response = jnp.einsum(
-        "vik,kj->vij", panels, conduction_cols[0], preferred_element_type=jnp.float32
-    ).astype(jnp.bfloat16)
-    valence_rows, gathered = gather(valence[None], response, None, 1)
-    kernel_sum = jnp.einsum(
-        "ik,vkj->vij", valence_rows[0], gathered, preferred_element_type=jnp.float32
-    )
-    kernel = masked(kernel_sum, mask_trial, row_index, col_index).astype(jnp.bfloat16)
+    vector_count, local_rows, local_cols = trial_vectors.shape
     row_blocks = local_rows // BS
     col_blocks = local_cols // BS
+    conduction = masked(p_conduction, mask_conduction, row_index, col_index)
+    trial_slots = block_slots(mask_trial, row_index, row_blocks, col_blocks)
+    valence_slots = block_slots(mask_valence, row_index, row_blocks, col_blocks)
+    trials = pack(trial_vectors, lax.dynamic_index_in_dim(trial_slots, col_index, 0, False))
+    valence = pack(p_valence[None], lax.dynamic_index_in_dim(valence_slots, col_index, 0, False))
+    trial_largest = largest_count(mask_trial, row_blocks, col_blocks)
+    valence_largest = largest_count(mask_valence, row_blocks, col_blocks)
+    keep = lax.dynamic_slice(
+        mask_trial, (row_index * row_blocks, col_index * col_blocks), (row_blocks, col_blocks)
+    )
+    panels, conduction_cols, partner = gather(
+        (8, 9, 10, 12, 16), trial_largest, 2, trials, conduction[None], orbitals
+    )
+    response = product(panels, trial_slots, conduction_cols, jnp.ones_like(keep))
+    valence_rows, gathered = gather((11, 12, 13, 16), valence_largest, 7, valence, response)
+    kernel = product(valence_rows, valence_slots, gathered, keep)
     starts_rows = lax.dynamic_slice_in_dim(sphere_starts, row_index * row_blocks, row_blocks, 0)
     starts_cols = lax.dynamic_slice_in_dim(sphere_starts, col_index * col_blocks, col_blocks, 0)
     slab_count = lax.axis_size("row") * lax.axis_size("col")
     density_grid = collocate(kernel, orbitals, partner, starts_rows, starts_cols, slab_count)
     n_row, n_col = lax.axis_size("row"), lax.axis_size("col")
     terms = density_grid.reshape(n_row, n_col, vector_count, SP)
-    density = reduce_over("col", reduce_over("row", terms, 2), 3)
+    density = reduce_over("col", reduce_over("row", terms, 0), 1)
     return (kernel, density)
 
 

time: 363 us -> 339 us (0.934)
  matrix products: 29.3 us -> 0 us
  Pallas kernels: 323 us -> 318 us
  between operations: 0.77 us -> 5.31 us
  local copies, waits for them, and re-layouts: 4.34 us -> 8.5 us
    dot_general x2 -> x0, matrix products: 29.3 us -> none  [the longest x1 14.6 us: local(): jnp.einsum('ik,vkj->vij', valence_rows[0], gathered, preferred_element_ty...]
    pallas_call x2 -> x6, Pallas kernels: 253 us -> 250 us  [the longest x2 202 us: gather_slots(): pl.pallas_call(functools.partial(gather_kernel, n_row, n_col, used, orbit...]
where the time goes in v3:
time: 339 us; the launch traced here: 338 us
  Pallas kernels  318 us (94%)
  local copies, waits for them, and re-layouts  8.5 us (3%)
  other arithmetic  5.4 us (2%)
  between operations  5.31 us (2%)
    pallas_call x2, Pallas kernels, gather_slots(): pl.pallas_call(functools.partial(gather_kernel, n_row, n_col, used, orbit...  202 us
    pallas_call x1, Pallas kernels, collocate(): pl.pallas_call(functools.partial(collocate_kernel, row_blocks, col_blocks...  56 us
    pallas_call x2, Pallas kernels, product(): pl.pallas_call(product_kernel, out_shape=jax.ShapeDtypeStruct((vectors, r...  44.6 us
    pallas_call x2, Pallas kernels, reduce_over(): pl.pallas_call(functools.partial(reduce_kernel, axis, size), out_shape=ja...  12.5 us

profile of v3, /device:TPU:0, one launch (start us, length us, event | category | flops | bytes accessed | tf_op | source)
XLA Modules:
  0.0 337.7 jit_solution(11993631190452362593)
XLA Ops:
  0.6 0.8 copy.34
  1.4 0.8 copy.41
  2.2 0.1 constant_dynamic-slice_fusion.1
  2.3 0.1 copy.44
  2.4 0.1 copy.45
  2.4 0.2 reduce_window_sum.18
  2.6 0.5 fusion.2.slots
  3.2 2.0 shard_map.96
  5.2 0.8 dynamic-slice_convert_fusion
  6.0 0.3 mul.28
  6.3 1.4 fusion
  7.7 0.1 reshape.60
  7.8 0.2 reduce_sum.19
  8.0 0.6 reduce_max.19
  11.2 116.5 %conditional.2 = ((bf16[8,2,4096,128]{3,2,1,0:T(8,128)(2,1)}, bf16[1,4096,512]{2,1,0:T(8,128)(2,1)}, bf16[4,128,8192]{2,1,0:T(8,128)(2,1)})) conditional(s32[]{:T(128)} %clamp.7, (bf16[2,4096,128]{2,1,0:T(8,128)(2,1)S(1)}, bf16[1,1024,512]{2,1,0:T(8,128)(2,1)S(1)}, bf16[8,128,8192]{2,1,0:T(8,128)(2,1)}) %tuple.35, ...), branch_computations={%region_6.7_spmd, %region_7.8_spmd, %region_8.9_spmd, %region_9.10... | conditional | bytes 8 | solution.py:289
  11.3 116.5 %branch_0_fun.2 = (bf16[8,2,4096,128]{3,2,1,0:T(8,128)(2,1)}, bf16[1,4096,512]{2,1,0:T(8,128)(2,1)}, bf16[4,128,8192]{2,1,0:T(8,128)(2,1)}) custom-call(bf16[2,4096,128]{2,1,0:T(8,128)(2,1)S(1)} %get-tuple-element.46.refs_0_, bf16[1,1024,512]{2,1,0:T(8,128)(2,1)S(1)} %get-tuple-element.47.refs_1_, bf16[8,128,8192]{2,1,0:T(8,128)(2,1)} %get-tuple-element.48.refs_2_), custom_call_target="tpu_custom_call" | custom-call | tf_op jit(solution)/shard_map/cond/branch_0_fun/pallas_call | solution.py:311
  127.8 0.1 sub.13
  127.9 0.1 copy.43
  128.0 0.1 gt.46
  128.1 0.6 broadcast_select_fusion.slots
  128.7 0.5 reshape.59.keep
  129.2 22.2 %shard_map.97 = bf16[2,1024,512]{2,1,0:T(8,128)(2,1)S(1)} custom-call(s32[256]{0:T(256)} %broadcast_select_fusion.slots, s32[32]{0:T(128)} %reshape.59.keep, bf16[8,2,4096,128]{3,2,1,0:T(8,128)(2,1)} %get-tuple-element.76.left_ref, bf16[1,4096,512]{2,1,0:T(8,128)(2,1)} %get-tuple-element.77.right_ref), custom_call_target="tpu_custom_call" | custom-call | tf_op jit(solution)/shard_map/pallas_call | solution.py:460
  151.4 0.1 copy.37
  151.5 0.1 copy.38
  151.6 0.2 reduce_window_sum.17
  151.8 0.5 fusion.1.slots
  152.3 1.6 shard_map.95
  153.9 0.1 reshape.56
  154.0 0.2 reduce_sum.18
  154.2 0.6 reduce_max.18
  156.8 85.3 %conditional.3 = ((bf16[8,1,4096,128]{3,2,1,0:T(8,128)(2,1)}, bf16[2,4096,512]{2,1,0:T(8,128)(2,1)})) conditional(s32[]{:T(128)} %clamp.6, (bf16[1,4096,128]{2,1,0:T(8,128)(2,1)S(1)}, bf16[2,1024,512]{2,1,0:T(8,128)(2,1)S(1)}) %tuple.36, (bf16[1,4096,128]{2,1,0:T(8,128)(2,1)S(1)}, ...), branch_computations={%region_11.12_spmd, %region_12.13_spmd, %region_13.14_spmd, %regio... | conditional | bytes 8 | solution.py:289
  156.8 85.0 %branch_0_fun.3 = (bf16[8,1,4096,128]{3,2,1,0:T(8,128)(2,1)}, bf16[2,4096,512]{2,1,0:T(8,128)(2,1)}) custom-call(bf16[1,4096,128]{2,1,0:T(8,128)(2,1)S(1)} %get-tuple-element.61.refs_0_, bf16[2,1024,512]{2,1,0:T(8,128)(2,1)S(1)} %get-tuple-element.62.refs_1_), custom_call_target="tpu_custom_call" | custom-call | tf_op jit(solution)/shard_map/cond/branch_0_fun/pallas_call | solution.py:311
  242.1 0.1 sub.11
  242.2 0.1 copy.36
  242.3 0.1 gt.40
  242.4 0.6 broadcast_select_fusion.1.slots
  243.0 0.8 dynamic_slice.26
  243.8 0.6 reshape.55.keep
  244.4 0.0 copy-start
  244.4 22.4 %shard_map.98.kernel_ref = bf16[2,1024,512]{2,1,0:T(8,128)(2,1)} custom-call(s32[256]{0:T(256)} %broadcast_select_fusion.1.slots, s32[32]{0:T(128)} %reshape.55.keep, bf16[8,1,4096,128]{3,2,1,0:T(8,128)(2,1)} %get-tuple-element.78.left_ref, bf16[2,4096,512]{2,1,0:T(8,128)(2,1)} %get-tuple-element.79.right_ref), custom_call_target="tpu_custom_call" | custom-call | tf_op jit(solution)/shard_map/pallas_call | solution.py:460
  266.8 0.0 copy-done
  266.8 0.6 dynamic_slice.32.starts_cols
  267.4 0.6 dynamic_slice.31.starts_rows
  267.9 56.0 %shard_map.99 = f32[32,2,512]{2,1,0:T(2,128)} custom-call(s32[8]{0:T(128)} %dynamic_slice.31.starts_rows, s32[4]{0:T(128)} %dynamic_slice.32.starts_cols, bf16[2,1024,512]{2,1,0:T(8,128)(2,1)} %shard_map.98.kernel_ref, bf16[8,128,8192]{2,1,0:T(8,128)(2,1)} %refs_7_.1, bf16[8,128,8192]{2,1,0:T(8,128)(2,1)} %refs_7_.1, bf16[8,128,8192]{2,1,0:T(8,128)(2,1)} %refs_7_.1, ...), custom_call_target="tpu_custom_call" | custom-call | tf_op jit(solution)/shard_map/pallas_call | solution.py:70
  324.0 5.1 %shard_map.100.in_ref = f32[8,2,512]{2,1,0:T(2,128)} custom-call(f32[4,8,2,512]{3,2,1,0:T(2,128)} %bitcast.34), custom_call_target="tpu_custom_call" | custom-call | tf_op jit(solution)/shard_map/pallas_call | solution.py:354
  329.0 7.4 %shard_map.101 = f32[2,512]{1,0:T(2,128)} custom-call(f32[8,2,512]{2,1,0:T(2,128)} %shard_map.100.in_ref), custom_call_target="tpu_custom_call" | custom-call | tf_op jit(solution)/shard_map/pallas_call | solution.py:354
  336.5 1.3 copy.82
  (6 shorter events, 0.0 us)
Async XLA Ops:
  244.4 22.4 %copy-start = (s32[32]{0:T(128)S(1)}, s32[32]{0:T(128)}, u32[]{:S(2)}) copy-start(s32[32]{0:T(128)} %param.24) | copy-start | bytes 388

commit v4 on v3

--- a/solution.py
+++ b/solution.py
@@ -23,64 +23,91 @@
     return (shaped * tile_mask[:, None, :, None]).reshape(values.shape)
 
 
-def collocate_kernel(row_blocks, col_blocks, starts_rows, starts_cols, kernel_ref, *refs):
+def collocate_kernel(row_blocks, col_blocks, starts_rows, starts_cols, keep, kernel_ref, *refs):
     row_refs = refs[:row_blocks]
     col_refs = refs[row_blocks : row_blocks + col_blocks]
     out_ref, frame_ref = refs[row_blocks + col_blocks :]
     slab = pl.program_id(0)
+    vectors = kernel_ref.shape[0]
+    group = 2 if col_blocks % 2 == 0 else 1
+    groups = col_blocks // group
+
+    def inside(start):
+        shift = slab - start
+        return ((shift >= 0) & (shift < SPAN)).astype(jnp.int32)
+
+    seen = [inside(starts_cols[j]) for j in range(col_blocks)]
     for j in range(col_blocks):
-        shift = slab - starts_cols[j]
-        active = (shift >= 0) & (shift < SPAN)
-
-        @pl.when(active)
+
+        @pl.when(seen[j] > 0)
         def _():
             frame_ref[j * BS : (j + 1) * BS, :] = col_refs[j][0]
 
-        @pl.when(jnp.logical_not(active))
+        @pl.when(seen[j] == 0)
         def _():
             frame_ref[j * BS : (j + 1) * BS, :] = jnp.zeros((BS, SP), frame_ref.dtype)
 
     out_ref[...] = jnp.zeros_like(out_ref)
     for i in range(row_blocks):
-        shift = slab - starts_rows[i]
-
-        @pl.when((shift >= 0) & (shift < SPAN))
-        def _():
-            own = row_refs[i][0].astype(jnp.float32)
-            vectors = kernel_ref.shape[0]
-            left = kernel_ref[:, i * BS : (i + 1) * BS, :].reshape(vectors * BS, col_blocks * BS)
-            applied = jnp.dot(left, frame_ref[...], preferred_element_type=jnp.float32)
-            for v in range(vectors):
-                term = own * applied[v * BS : (v + 1) * BS]
-                out_ref[0, v : v + 1, :] += jnp.sum(term, axis=0, keepdims=True)
-
-
-def orbital_spec(block, which):
-    def index_map(slab, starts_rows, starts_cols):
+        needed = []
+        for g in range(groups):
+            uses = sum(seen[j] * keep[i * col_blocks + j] for j in range(g * group, (g + 1) * group))
+            needed.append((inside(starts_rows[i]) > 0) & (uses > 0))
+        for lo in range(groups):
+            for hi in range(lo + 1, groups + 1):
+                chosen = needed[lo] & needed[hi - 1]
+                for g in range(groups):
+                    if g < lo or g >= hi:
+                        chosen = chosen & jnp.logical_not(needed[g])
+
+                @pl.when(chosen)
+                def _():
+                    own = row_refs[i][0].astype(jnp.float32)
+                    deep = slice(lo * group * BS, hi * group * BS)
+                    left = kernel_ref[:, i * BS : (i + 1) * BS, deep]
+                    left = left.reshape(vectors * BS, (hi - lo) * group * BS)
+                    applied = jnp.dot(
+                        left, frame_ref[deep, :], preferred_element_type=jnp.float32
+                    )
+                    for v in range(vectors):
+                        term = own * applied[v * BS : (v + 1) * BS]
+                        out_ref[0, v : v + 1, :] += jnp.sum(term, axis=0, keepdims=True)
+
+
+def orbital_spec(block, place, which):
+    def index_map(slab, starts_rows, starts_cols, keep):
         start = (starts_rows, starts_cols)[which][block]
-        return block, 0, jnp.clip(slab - start, 0, SPAN - 1)
+        return place, 0, jnp.clip(slab - start, 0, SPAN - 1)
 
     return pl.BlockSpec((1, BS, SP), index_map)
 
 
-def collocate(kernel, orbitals, partner, starts_rows, starts_cols, slab_count):
+def collocate(kernel, keep, orbitals, partners, starts_rows, starts_cols, slab_count):
     vector_count = kernel.shape[0]
     row_blocks = orbitals.shape[0]
-    col_blocks = partner.shape[0]
+    places = [(part, k) for part in partners for k in range(part.shape[0])]
+    col_blocks = len(places)
     return pl.pallas_call(
         functools.partial(collocate_kernel, row_blocks, col_blocks),
         out_shape=jax.ShapeDtypeStruct((slab_count, vector_count, SP), jnp.float32),
         grid_spec=pltpu.PrefetchScalarGridSpec(
-            num_scalar_prefetch=2,
+            num_scalar_prefetch=3,
             grid=(slab_count,),
-            in_specs=[pl.BlockSpec(kernel.shape, lambda slab, a, b: (0, 0, 0))]
-            + [orbital_spec(i, 0) for i in range(row_blocks)]
-            + [orbital_spec(j, 1) for j in range(col_blocks)],
-            out_specs=pl.BlockSpec((1, vector_count, SP), lambda slab, a, b: (slab, 0, 0)),
+            in_specs=[pl.BlockSpec(kernel.shape, lambda slab, a, b, c: (0, 0, 0))]
+            + [orbital_spec(i, i, 0) for i in range(row_blocks)]
+            + [orbital_spec(j, places[j][1], 1) for j in range(col_blocks)],
+            out_specs=pl.BlockSpec((1, vector_count, SP), lambda slab, a, b, c: (slab, 0, 0)),
             scratch_shapes=[pltpu.VMEM((col_blocks * BS, SP), jnp.bfloat16)],
         ),
         compiler_params=pltpu.CompilerParams(dimension_semantics=("arbitrary",)),
-    )(starts_rows, starts_cols, kernel, *([orbitals] * row_blocks), *([partner] * col_blocks))
+    )(
+        starts_rows,
+        starts_cols,
+        keep.reshape(-1),
+        kernel,
+        *([orbitals] * row_blocks),
+        *[part for part, _ in places],
+    )
 
 
 def ring_place(col, size):
@@ -119,7 +146,7 @@
     return stack.at[:, pl.ds(pl.multiple_of(row * rows, rows), rows), :]
 
 
-def gather_kernel(n_row, n_col, used, with_orbitals, *refs):
+def gather_kernel(n_row, n_col, used, span, with_orbitals, *refs):
     refs = list(refs)
     ring_in, row_in = refs[:2]
     del refs[:2]
@@ -178,38 +205,43 @@
     across(0).start()
 
     if with_orbitals:
-        blocks = partner.shape[0]
-        part = blocks // 2
+        offset, count, blocks = span
+        part = partner.shape[1] // 2
         ratio = n_col // n_row
         source = col // ratio
-        own = orbitals.at[pl.ds(col % ratio * blocks, blocks)]
+        first = col % ratio * blocks + offset
+        own = orbitals.at[pl.ds(first, count)]
         here = chip == source // 2
         is_source = row == source
 
         def to_pair():
             return remote(own, partner, orbital_send.at[0], orbital_recv.at[0], row=pair)
 
-        def to_chip(d, h):
-            k = 1 + 2 * (d - 1) + h
+        def to_chip(d, h, k):
             return remote(
-                orbitals.at[pl.ds(col % ratio * blocks + h * part, part)],
-                partner.at[pl.ds(h * part, part)],
-                orbital_send.at[k],
-                orbital_recv.at[1],
+                orbitals.at[pl.ds(first + k, 1), pl.ds(h * part, part)],
+                partner.at[pl.ds(k, 1), pl.ds(h * part, part)],
+                orbital_send.at[1 + (2 * (d - 1) + h) * count + k],
+                orbital_recv.at[1 + k],
                 row=(chip + d) % chips * 2 + h,
             )
 
-        def half_onward():
-            held = partner.at[pl.ds(core * part, part)]
+        def half_onward(k):
+            held = partner.at[pl.ds(k, 1), pl.ds(pl.multiple_of(core * part, part), part)]
             return remote(
-                held, held, orbital_send.at[2 * chips - 1], orbital_recv.at[2], row=pair
+                held,
+                held,
+                orbital_send.at[1 + 2 * (chips - 1) * count + k],
+                orbital_recv.at[1 + count + k],
+                row=pair,
             )
 
         @pl.when(is_source)
         def _():
-            for d in range(1, chips):
-                for h in range(2):
-                    to_chip(d, h).start()
+            for k in range(count):
+                for d in range(1, chips):
+                    for h in range(2):
+                        to_chip(d, h, k).start()
             to_pair().start()
 
     ins = [(ring_in.at[:, pl.ds(0, used), :], ring_hold), (row_in, row_hold)]
@@ -236,16 +268,18 @@
             ring(step, way).wait_recv()
             if step < n_col - 2:
                 ring(step + 1, way).start()
-        if step == min(2, n_col - 2):
+        if step == n_col - 3:
             for d in range(1, chips):
                 across(d).wait_recv()
                 onward(d).start()
-        if with_orbitals and step == n_col - 3:
-
-            @pl.when(jnp.logical_not(here))
-            def _():
-                to_chip(1, 0).wait_recv()
-                half_onward().start()
+
+    if with_orbitals:
+
+        @pl.when(jnp.logical_not(here))
+        def _():
+            for k in range(count):
+                to_chip(1, 0, k).wait_recv()
+                half_onward(k).start()
 
     across(0).wait_recv()
     for d in range(1, chips):
@@ -259,7 +293,8 @@
         def _():
             for d in range(1, chips):
                 for h in range(2):
-                    to_chip(d, h).wait_send()
+                    for k in range(count):
+                        to_chip(d, h, k).wait_send()
             to_pair().wait_send()
             pltpu.make_async_copy(orbital_hold, partner, hold_out.at[2]).wait()
 
@@ -269,8 +304,9 @@
 
         @pl.when(jnp.logical_not(here))
         def _():
-            half_onward().wait_recv()
-            half_onward().wait_send()
+            for k in range(count):
+                half_onward(k).wait_recv()
+                half_onward(k).wait_send()
 
     for step in range(n_col - 1):
         for way in range(2):
@@ -279,17 +315,17 @@
         pltpu.make_async_copy(*outs[k], hold_out.at[k]).wait()
 
 
-def gather(fractions, largest, first_id, *arrays):
+def gather(fractions, largest, first_id, span, *arrays):
     slots = arrays[0].shape[1] // BS
     caps = sorted({-(-slots * part // 16) for part in fractions})
     branches = [
-        functools.partial(gather_slots, cap * BS, first_id + k) for k, cap in enumerate(caps)
+        functools.partial(gather_slots, cap * BS, first_id + k, span) for k, cap in enumerate(caps)
     ]
     index = sum((largest > cap).astype(jnp.int32) for cap in caps[:-1])
     return lax.switch(index, branches, *arrays)
 
 
-def gather_slots(used, collective_id, ring_in, row_in, orbitals=None):
+def gather_slots(used, collective_id, span, ring_in, row_in, orbitals=None):
     n_row, n_col = lax.axis_size("row"), lax.axis_size("col")
     panel = jax.ShapeDtypeStruct((n_col,) + ring_in.shape, ring_in.dtype)
     stack = jax.ShapeDtypeStruct(
@@ -302,14 +338,14 @@
     sems = [dma((3,)), dma((3,)), dma((2, n_col - 1)), dma((2, n_col - 1))]
     sems += [dma((n_row - 1,)), dma((n_row - 1,))]
     if orbitals is not None:
-        blocks = orbitals.shape[0] * n_row // n_col
-        partner = (blocks,) + orbitals.shape[1:]
+        count, chips = span[1], n_row // 2
+        partner = (count,) + orbitals.shape[1:]
         operands.append(orbitals)
         results.append(jax.ShapeDtypeStruct(partner, orbitals.dtype))
         holds.append(pltpu.VMEM(partner, orbitals.dtype))
-        sems += [dma((n_row,)), dma((3,))]
+        sems += [dma((1 + (2 * chips - 1) * count,)), dma((1 + 2 * count,))]
     return pl.pallas_call(
-        functools.partial(gather_kernel, n_row, n_col, used, orbitals is not None),
+        functools.partial(gather_kernel, n_row, n_col, used, span, orbitals is not None),
         out_shape=results,
         in_specs=[pl.BlockSpec(memory_space=pl.ANY)] * len(operands),
         out_specs=[pl.BlockSpec(memory_space=pl.ANY)] * len(results),
@@ -502,16 +538,33 @@
     keep = lax.dynamic_slice(
         mask_trial, (row_index * row_blocks, col_index * col_blocks), (row_blocks, col_blocks)
     )
-    panels, conduction_cols, partner = gather(
-        (8, 9, 10, 12, 16), trial_largest, 2, trials, conduction[None], orbitals
+    early = max(1, col_blocks * 3 // 4)
+    panels, conduction_cols, partner_early = gather(
+        (8, 9, 10, 12, 16),
+        trial_largest,
+        2,
+        (0, early, col_blocks),
+        trials,
+        conduction[None],
+        orbitals,
     )
     response = product(panels, trial_slots, conduction_cols, jnp.ones_like(keep))
-    valence_rows, gathered = gather((11, 12, 13, 16), valence_largest, 7, valence, response)
+    valence_rows, gathered, partner_late = gather(
+        (11, 12, 13, 16),
+        valence_largest,
+        7,
+        (early, col_blocks - early, col_blocks),
+        valence,
+        response,
+        orbitals,
+    )
     kernel = product(valence_rows, valence_slots, gathered, keep)
     starts_rows = lax.dynamic_slice_in_dim(sphere_starts, row_index * row_blocks, row_blocks, 0)
     starts_cols = lax.dynamic_slice_in_dim(sphere_starts, col_index * col_blocks, col_blocks, 0)
     slab_count = lax.axis_size("row") * lax.axis_size("col")
-    density_grid = collocate(kernel, orbitals, partner, starts_rows, starts_cols, slab_count)
+    density_grid = collocate(
+        kernel, keep, orbitals, (partner_early, partner_late), starts_rows, starts_cols, slab_count
+    )
     n_row, n_col = lax.axis_size("row"), lax.axis_size("col")
     terms = density_grid.reshape(n_row, n_col, vector_count, SP)
     density = reduce_over("col", reduce_over("row", terms, 0), 1)

time: 339 us -> 305 us (0.90); the launches traced: 338 us -> 299 us
  Pallas kernels: 318 us -> 280 us
    pallas_call x2, Pallas kernels: 202 us -> 170 us  [gather_slots(): pl.pallas_call(functools.partial(gather_kernel, n_row, n_col, used, span,...]
    pallas_call x1, Pallas kernels: 56 us -> 44.4 us  [collocate(): pl.pallas_call(functools.partial(collocate_kernel, row_blocks, col_blocks...]
    pallas_call x2, Pallas kernels: 12.5 us -> 17.1 us  [reduce_over(): pl.pallas_call(functools.partial(reduce_kernel, axis, size), out_shape=ja...]
where the time goes in v4:
time: 305 us; the launch traced here: 299 us
  Pallas kernels  280 us (92%)
  local copies, waits for them, and re-layouts  8.51 us (3%)
  other arithmetic  5.4 us (2%)
  between operations  5.31 us (2%)
    pallas_call x2, Pallas kernels, gather_slots(): pl.pallas_call(functools.partial(gather_kernel, n_row, n_col, used, span,...  170 us
    pallas_call x2, Pallas kernels, product(): pl.pallas_call(product_kernel, out_shape=jax.ShapeDtypeStruct((vectors, r...  44.6 us
    pallas_call x1, Pallas kernels, collocate(): pl.pallas_call(functools.partial(collocate_kernel, row_blocks, col_blocks...  44.4 us
    pallas_call x2, Pallas kernels, reduce_over(): pl.pallas_call(functools.partial(reduce_kernel, axis, size), out_shape=ja...  17.1 us

profile of v4, /device:TPU:0, one launch (start us, length us, event | category | flops | bytes accessed | tf_op | source)
XLA Modules:
  0.0 299.3 jit_solution(12047103693863310260)
XLA Ops:
  0.6 0.8 copy.34
  1.4 0.8 copy.41
  2.2 0.1 constant_dynamic-slice_fusion.1
  2.3 0.1 copy.44
  2.4 0.1 copy.45
  2.4 0.2 reduce_window_sum.18
  2.6 0.5 fusion.2.slots
  3.2 2.0 shard_map.96
  5.2 0.8 dynamic-slice_convert_fusion
  6.0 0.3 mul.28
  6.3 1.4 fusion
  7.7 0.1 reshape.61
  7.8 0.2 reduce_sum.19
  8.0 0.6 reduce_max.19
  11.2 94.1 %conditional.2 = ((bf16[8,2,4096,128]{3,2,1,0:T(8,128)(2,1)}, bf16[1,4096,512]{2,1,0:T(8,128)(2,1)}, bf16[3,128,8192]{2,1,0:T(8,128)(2,1)})) conditional(s32[]{:T(128)} %clamp.7, (bf16[2,4096,128]{2,1,0:T(8,128)(2,1)S(1)}, bf16[1,1024,512]{2,1,0:T(8,128)(2,1)S(1)}, bf16[8,128,8192]{2,1,0:T(8,128)(2,1)}) %tuple.35, ...), branch_computations={%region_6.7_spmd, %region_7.8_spmd, %region_8.9_spmd, %region_9.10... | conditional | bytes 8 | solution.py:325
  11.2 94.1 %branch_0_fun.2 = (bf16[8,2,4096,128]{3,2,1,0:T(8,128)(2,1)}, bf16[1,4096,512]{2,1,0:T(8,128)(2,1)}, bf16[3,128,8192]{2,1,0:T(8,128)(2,1)}) custom-call(bf16[2,4096,128]{2,1,0:T(8,128)(2,1)S(1)} %get-tuple-element.54.refs_0_, bf16[1,1024,512]{2,1,0:T(8,128)(2,1)S(1)} %get-tuple-element.55.refs_1_, bf16[8,128,8192]{2,1,0:T(8,128)(2,1)} %get-tuple-element.56.refs_2_), custom_call_target="tpu_custom_call" | custom-call | tf_op jit(solution)/shard_map/cond/branch_0_fun/pallas_call | solution.py:347
  105.4 0.1 sub.13
  105.5 0.1 copy.43
  105.6 0.1 gt.46
  105.7 0.6 broadcast_select_fusion.slots
  106.3 0.5 reshape.60.keep
  106.8 22.1 %shard_map.97 = bf16[2,1024,512]{2,1,0:T(8,128)(2,1)S(1)} custom-call(s32[256]{0:T(256)} %broadcast_select_fusion.slots, s32[32]{0:T(128)} %reshape.60.keep, bf16[8,2,4096,128]{3,2,1,0:T(8,128)(2,1)} %get-tuple-element.89.left_ref, bf16[1,4096,512]{2,1,0:T(8,128)(2,1)} %get-tuple-element.90.right_ref), custom_call_target="tpu_custom_call" | custom-call | tf_op jit(solution)/shard_map/pallas_call | solution.py:496
  128.9 0.1 copy.37
  129.0 0.1 copy.38
  129.1 0.2 reduce_window_sum.17
  129.3 0.5 fusion.1.slots
  129.8 1.6 shard_map.95
  131.4 0.1 reshape.57
  131.5 0.2 reduce_sum.18
  131.7 0.6 reduce_max.18
  134.3 76.3 %conditional.3 = ((bf16[8,1,4096,128]{3,2,1,0:T(8,128)(2,1)}, bf16[2,4096,512]{2,1,0:T(8,128)(2,1)}, bf16[1,128,8192]{2,1,0:T(8,128)(2,1)})) conditional(s32[]{:T(128)} %clamp.6, (bf16[1,4096,128]{2,1,0:T(8,128)(2,1)S(1)}, bf16[2,1024,512]{2,1,0:T(8,128)(2,1)S(1)}, bf16[8,128,8192]{2,1,0:T(8,128)(2,1)}) %tuple.36, ...), branch_computations={%region_11.12_spmd, %region_12.13_spmd, %region_13.14_spmd, %regio... | conditional | bytes 8 | solution.py:325
  134.3 76.1 %branch_2_fun.3 = (bf16[8,1,4096,128]{3,2,1,0:T(8,128)(2,1)}, bf16[2,4096,512]{2,1,0:T(8,128)(2,1)}, bf16[1,128,8192]{2,1,0:T(8,128)(2,1)}) custom-call(bf16[1,4096,128]{2,1,0:T(8,128)(2,1)S(1)} %get-tuple-element.75.refs_0_, bf16[2,1024,512]{2,1,0:T(8,128)(2,1)S(1)} %get-tuple-element.76.refs_1_, bf16[8,128,8192]{2,1,0:T(8,128)(2,1)} %get-tuple-element.77.refs_2_), custom_call_target="tpu_custom_call" | custom-call | tf_op jit(solution)/shard_map/cond/branch_2_fun/pallas_call | solution.py:347
  210.6 0.1 sub.11
  210.7 0.1 copy.36
  210.8 0.1 gt.40
  211.0 0.6 broadcast_select_fusion.1.slots
  211.5 0.8 dynamic_slice.26
  212.3 0.6 reshape.56.keep
  212.9 0.0 copy-start.1
  212.9 0.0 copy-start
  212.9 22.5 %shard_map.98.kernel_ref = bf16[2,1024,512]{2,1,0:T(8,128)(2,1)} custom-call(s32[256]{0:T(256)} %broadcast_select_fusion.1.slots, s32[32]{0:T(128)} %reshape.56.keep, bf16[8,1,4096,128]{3,2,1,0:T(8,128)(2,1)} %get-tuple-element.91.left_ref, bf16[2,4096,512]{2,1,0:T(8,128)(2,1)} %get-tuple-element.92.right_ref), custom_call_target="tpu_custom_call" | custom-call | tf_op jit(solution)/shard_map/pallas_call | solution.py:496
  235.4 0.0 copy-done.1
  235.4 0.6 dynamic_slice.32.starts_cols
  236.0 0.6 dynamic_slice.31.starts_rows
  236.5 0.0 copy-done
  236.5 44.4 %shard_map.99 = f32[32,2,512]{2,1,0:T(2,128)} custom-call(s32[8]{0:T(128)} %dynamic_slice.31.starts_rows, s32[4]{0:T(128)} %dynamic_slice.32.starts_cols, s32[32]{0:T(128)} %reshape.56.keep, bf16[2,1024,512]{2,1,0:T(8,128)(2,1)} %shard_map.98.kernel_ref, bf16[8,128,8192]{2,1,0:T(8,128)(2,1)} %refs_7_.1, bf16[8,128,8192]{2,1,0:T(8,128)(2,1)} %refs_7_.1, ...), custom_call_target="tpu_custom_call" | custom-call | tf_op jit(solution)/shard_map/pallas_call | solution.py:90
  280.9 8.3 %shard_map.100.in_ref = f32[8,2,512]{2,1,0:T(2,128)} custom-call(f32[4,8,2,512]{3,2,1,0:T(2,128)} %bitcast.34), custom_call_target="tpu_custom_call" | custom-call | tf_op jit(solution)/shard_map/pallas_call | solution.py:390
  289.2 8.8 %shard_map.101 = f32[2,512]{1,0:T(2,128)} custom-call(f32[8,2,512]{2,1,0:T(2,128)} %shard_map.100.in_ref), custom_call_target="tpu_custom_call" | custom-call | tf_op jit(solution)/shard_map/pallas_call | solution.py:390
  298.0 1.3 copy.86
  (6 shorter events, 0.0 us)
Async XLA Ops:
  212.9 22.5 %copy-start.1 = (s32[32]{0:T(128)S(1)}, s32[32]{0:T(128)}, u32[]{:S(2)}) copy-start(s32[32]{0:T(128)} %param.24) | copy-start | bytes 388
  212.9 23.6 %copy-start = (bf16[1,128,8192]{2,1,0:T(8,128)(2,1)S(1)}, bf16[1,128,8192]{2,1,0:T(8,128)(2,1)}, u32[]{:S(2)}) copy-start(bf16[1,128,8192]{2,1,0:T(8,128)(2,1)} %get-tuple-element.94.refs_11_) | copy-start | bytes 6291460
